TPU v7x, 32 devices: a whole 2x2x4 slice. The times are simulated.
32 devices in a mesh: batch: 4 (over y, core), blk: 8 (over z, x).
Axes of the slice: x: 2, y: 2, z: 4, core: 2. Of those that a mesh axis runs over, the one named last changes fastest.
Arguments:
- inputs: bfloat16 [2, 4, 1024, 1024], P(None, 'batch', 'blk'), may hold values from -6 to 6
- segment_ids: int32 [2, 4, 1024], P(None, 'batch', 'blk'), may hold values from 0 to 3, never falling along the last dimension, each value on 1 to 640 neighbouring positions
- cotangent: bfloat16 [2, 4, 1024, 1024], P(None, 'batch', 'blk'), may hold values from -6 to 6
- qkv_weight: bfloat16 [1024, 3072], P(('batch', 'blk')), may hold values from -0.1875 to 0.1875
- out_weight: bfloat16 [1024, 1024], P(('batch', 'blk')), may hold values from -0.75 to 0.75
- up_weight: bfloat16 [1024, 4096], P(('batch', 'blk')), may hold values from -0.1875 to 0.1875
- down_weight: bfloat16 [4096, 1024], P(('batch', 'blk')), may hold values from -0.09375 to 0.09375
- first_gain: bfloat16 [1024], P(('batch', 'blk')), may hold values from 0.5 to 1.5
- first_bias: bfloat16 [1024], P(('batch', 'blk')), may hold values from -4 to 4
- second_gain: bfloat16 [1024], P(('batch', 'blk')), may hold values from 0.5 to 1.5
- second_bias: bfloat16 [1024], P(('batch', 'blk')), may hold values from -4 to 4
- out_bias: bfloat16 [1024], P(('batch', 'blk')), may hold values from -4 to 4
- up_bias: bfloat16 [4096], P(('batch', 'blk')), may hold values from -4 to 4
- down_bias: bfloat16 [1024], P(('batch', 'blk')), may hold values from -4 to 4
Outputs:
- result: float32 [2, 4, 1024, 1024], P(None, 'batch', 'blk')
- input_grad: float32 [2, 4, 1024, 1024], P(None, 'batch', 'blk')
- qkv_grad: float32 [1024, 3072], P(('batch', 'blk'))
- out_grad: float32 [1024, 1024], P(('batch', 'blk'))
- up_grad: float32 [1024, 4096], P(('batch', 'blk'))
- down_grad: float32 [4096, 1024], P(('batch', 'blk'))
- first_gain_grad: float32 [1024], P(('batch', 'blk'))
- first_bias_grad: float32 [1024], P(('batch', 'blk'))
- second_gain_grad: float32 [1024], P(('batch', 'blk'))
- second_bias_grad: float32 [1024], P(('batch', 'blk'))
- out_bias_grad: float32 [1024], P(('batch', 'blk'))
- up_bias_grad: float32 [4096], P(('batch', 'blk'))
- down_bias_grad: float32 [1024], P(('batch', 'blk'))
Inputs may be any that keep to these rules, and one draw needn't show every extreme that they name: `segment_ids`: along each set the ids never fall; each image holds 1 to 640 latents, and one image of every set holds exactly 640.
All inputs are finite; a program needn't handle non-finite values.
Results may differ from a plain program's by a relative error of at most 0.025.
Values may be sent and summed in bfloat16 or wider, within the bound.
No kernel may reach another device: no remote copies, remote signals or barrier semaphores. Data moves between devices by JAX's collectives and lax.ppermute only.
A program may use at most 320 MiB of HBM per device.

v0:
```python
from functools import partial

import jax
import jax.numpy as jnp
from jax import lax
from jax.experimental import pallas as pl
from jax.experimental.pallas import tpu as pltpu
from jax.sharding import PartitionSpec as P

H = 8


epsilon = 1e-05
masked_score = -1e30


def dense(former, latter):
    return jnp.dot(former, latter, preferred_element_type=jnp.float32)


def norm_rows(values, gains, shifts):
    average = jnp.mean(values, axis=-1, keepdims=True)
    centred = values - average
    inverse = lax.rsqrt(jnp.mean(centred * centred, axis=-1, keepdims=True) + epsilon)
    scaled = centred * inverse
    return (scaled * gains + shifts, scaled, inverse)


def norm_back(gradient, scaled, inverse, gains):
    upstream = gradient * gains
    return inverse * (
        upstream
        - jnp.mean(upstream, axis=-1, keepdims=True)
        - scaled * jnp.mean(upstream * scaled, axis=-1, keepdims=True)
    )


def block_scan(update, carried, pieces):
    amount = pieces[0].shape[1]
    stride = min(512, amount)

    def block_step(state_now, number):
        sliced = tuple(
            (lax.dynamic_slice_in_dim(member, number * stride, stride, 1) for member in pieces)
        )
        return (update(state_now, sliced), None)

    carried, unused = lax.scan(block_step, carried, jnp.arange(amount // stride))
    return carried


def split_heads(rows, head_count):
    return rows.reshape(rows.shape[0], rows.shape[1], head_count, rows.shape[2] // head_count)


def attend_piece(running, sliced, queries, query_segs):
    maximum, totals, accumulated = running
    key_part, value_part, seg_part = sliced
    head_count, head_size = (queries.shape[2], queries.shape[3])
    key_heads = split_heads(key_part, head_count)
    value_heads = split_heads(value_part, head_count)
    scores = jnp.einsum(
        "sqhd,skhd->shqk", queries, key_heads, preferred_element_type=jnp.float32
    ) * head_size ** (-0.5)
    allowed = query_segs[:, None, :, None] == seg_part[:, None, None, :]
    scores = jnp.where(allowed, scores, masked_score)
    highest = jnp.maximum(maximum, jnp.max(scores, axis=-1, keepdims=True))
    factor = jnp.exp(maximum - highest)
    shares = jnp.exp(scores - highest)
    totals = totals * factor + jnp.sum(shares, axis=-1, keepdims=True)
    accumulated = accumulated * factor + jnp.einsum(
        "shqk,skhd->shqd",
        shares.astype(jnp.bfloat16),
        value_heads,
        preferred_element_type=jnp.float32,
    )
    return (highest, totals, accumulated)


def fold_keys(running, pieces, queries, query_segs):
    return block_scan(
        partial(attend_piece, queries=queries, query_segs=query_segs), running, pieces
    )


def grad_block(queries, grad_heads, query_segs, log_total, delta, key_heads, value_heads, key_segs):
    head_size = queries.shape[3]
    scores = jnp.einsum(
        "sqhd,skhd->shqk", queries, key_heads, preferred_element_type=jnp.float32
    ) * head_size ** (-0.5)
    allowed = query_segs[:, None, :, None] == key_segs[:, None, None, :]
    shares = jnp.where(allowed, jnp.exp(scores - log_total), 0.0)
    grad_shares = jnp.einsum(
        "sqhd,skhd->shqk", grad_heads, value_heads, preferred_element_type=jnp.float32
    )
    grad_scores = (shares * (grad_shares - delta)).astype(jnp.bfloat16)
    return (shares.astype(jnp.bfloat16), grad_scores)


def micro_step(set_inputs, set_segs, set_cotangent, gathered):
    (
        weight_qkv,
        weight_out,
        weight_up,
        weight_down,
        gain_one,
        shift_one,
        gain_two,
        shift_two,
        bias_out,
        bias_up,
        bias_down,
    ) = gathered
    set_count, tok_count, features = set_inputs.shape
    head_count = H
    head_size = features // head_count
    scale = head_size ** (-0.5)
    rows = set_inputs.astype(jnp.float32).reshape(-1, features)
    normed, scaled_one, inverse_one = norm_rows(
        rows, gain_one.astype(jnp.float32), shift_one.astype(jnp.float32)
    )
    normed_low = normed.astype(jnp.bfloat16)
    mixed = dense(normed_low, weight_qkv).astype(jnp.bfloat16)
    queries = mixed[:, :features].reshape(set_count, tok_count, head_count, head_size)
    key_rows = mixed[:, features : 2 * features].reshape(set_count, tok_count, features)
    value_rows = mixed[:, 2 * features :].reshape(set_count, tok_count, features)
    running = (
        jnp.full((set_count, head_count, tok_count, 1), masked_score, jnp.float32),
        jnp.zeros((set_count, head_count, tok_count, 1), jnp.float32),
        jnp.zeros((set_count, head_count, tok_count, head_size), jnp.float32),
    )
    running = fold_keys(
        running,
        (
            lax.all_gather(key_rows, "blk", axis=1, tiled=True),
            lax.all_gather(value_rows, "blk", axis=1, tiled=True),
            lax.all_gather(set_segs, "blk", axis=1, tiled=True),
        ),
        queries=queries,
        query_segs=set_segs,
    )
    maximum, totals, accumulated = running
    attended = accumulated / totals
    log_total = maximum + jnp.log(totals)
    attended_low = jnp.transpose(attended, (0, 2, 1, 3)).reshape(-1, features).astype(jnp.bfloat16)
    middle = rows + dense(attended_low, weight_out) + bias_out.astype(jnp.float32)
    normed_two, scaled_two, inverse_two = norm_rows(
        middle, gain_two.astype(jnp.float32), shift_two.astype(jnp.float32)
    )
    normed_two_low = normed_two.astype(jnp.bfloat16)
    upper = dense(normed_two_low, weight_up) + bias_up.astype(jnp.float32)
    activ_value, gelu_back = jax.vjp(lambda v: jax.nn.gelu(v, approximate=False), upper)
    activ_low = activ_value.astype(jnp.bfloat16)
    final = middle + dense(activ_low, weight_down) + bias_down.astype(jnp.float32)
    grad_out = set_cotangent.astype(jnp.float32).reshape(-1, features)
    grad_low = grad_out.astype(jnp.bfloat16)
    grad_down_bias = jnp.sum(grad_low.astype(jnp.float32), axis=0)
    grad_down = jnp.einsum("rf,rd->fd", activ_low, grad_low, preferred_element_type=jnp.float32)
    grad_activ = jnp.einsum("rd,fd->rf", grad_low, weight_down, preferred_element_type=jnp.float32)
    grad_upper = gelu_back(grad_activ)[0].astype(jnp.bfloat16)
    grad_up_bias = jnp.sum(grad_upper.astype(jnp.float32), axis=0)
    grad_up = jnp.einsum(
        "rd,rf->df", normed_two_low, grad_upper, preferred_element_type=jnp.float32
    )
    grad_normed_two = jnp.einsum(
        "rf,df->rd", grad_upper, weight_up, preferred_element_type=jnp.float32
    )
    grad_gain_two = jnp.sum(grad_normed_two * scaled_two, axis=0)
    grad_shift_two = jnp.sum(grad_normed_two, axis=0)
    grad_middle = grad_out + norm_back(
        grad_normed_two, scaled_two, inverse_two, gain_two.astype(jnp.float32)
    )
    branch_low = grad_middle.astype(jnp.bfloat16)
    grad_out_bias = jnp.sum(branch_low.astype(jnp.float32), axis=0)
    grad_out_weight = jnp.einsum(
        "rd,re->de", attended_low, branch_low, preferred_element_type=jnp.float32
    )
    grad_attended = jnp.einsum(
        "re,de->rd", branch_low, weight_out, preferred_element_type=jnp.float32
    )
    grad_heads = grad_attended.astype(jnp.bfloat16).reshape(
        set_count, tok_count, head_count, head_size
    )
    delta = jnp.einsum("sqhd,shqd->shq", grad_heads.astype(jnp.float32), attended)[..., None]
    everything = (
        lax.all_gather(key_rows, "blk", axis=1, tiled=True),
        lax.all_gather(value_rows, "blk", axis=1, tiled=True),
        lax.all_gather(set_segs, "blk", axis=1, tiled=True),
    )
    length = everything[0].shape[1]
    stride = min(512, length)

    def key_block(grad_query, number):
        key_part = lax.dynamic_slice_in_dim(everything[0], number * stride, stride, 1)
        value_part = lax.dynamic_slice_in_dim(everything[1], number * stride, stride, 1)
        seg_part = lax.dynamic_slice_in_dim(everything[2], number * stride, stride, 1)
        key_heads = split_heads(key_part, head_count)
        share_low, score_low = grad_block(
            queries,
            grad_heads,
            set_segs,
            log_total,
            delta,
            key_heads,
            split_heads(value_part, head_count),
            seg_part,
        )
        grad_query = (
            grad_query
            + jnp.einsum(
                "shqk,skhd->sqhd", score_low, key_heads, preferred_element_type=jnp.float32
            )
            * scale
        )
        key_term = (
            jnp.einsum("shqk,sqhd->kshd", score_low, queries, preferred_element_type=jnp.float32)
            * scale
        )
        value_term = jnp.einsum(
            "shqk,sqhd->kshd", share_low, grad_heads, preferred_element_type=jnp.float32
        )
        return (
            grad_query,
            jnp.concatenate(
                (
                    key_term.reshape(stride, set_count, features),
                    value_term.reshape(stride, set_count, features),
                ),
                axis=-1,
            ),
        )

    grad_query, terms = lax.scan(
        key_block, jnp.zeros(queries.shape, jnp.float32), jnp.arange(length // stride)
    )
    summed = lax.psum_scatter(
        terms.reshape(length, set_count, 2 * features).astype(jnp.bfloat16),
        "blk",
        scatter_dimension=0,
        tiled=True,
    ).astype(jnp.float32)
    summed = jnp.transpose(summed, (1, 0, 2)).reshape(-1, 2 * features)
    grad_keys = summed[:, :features]
    grad_values = summed[:, features:]
    grad_mixed = jnp.concatenate(
        (grad_query.reshape(-1, features), grad_keys, grad_values), axis=-1
    ).astype(jnp.bfloat16)
    grad_qkv = jnp.einsum("rd,re->de", normed_low, grad_mixed, preferred_element_type=jnp.float32)
    grad_normed = jnp.einsum(
        "re,de->rd", grad_mixed, weight_qkv, preferred_element_type=jnp.float32
    )
    grad_gain_one = jnp.sum(grad_normed * scaled_one, axis=0)
    grad_shift_one = jnp.sum(grad_normed, axis=0)
    grad_input = grad_middle + norm_back(
        grad_normed, scaled_one, inverse_one, gain_one.astype(jnp.float32)
    )
    local_grads = (
        grad_qkv,
        grad_out_weight,
        grad_up,
        grad_down,
        grad_gain_one,
        grad_shift_one,
        grad_gain_two,
        grad_shift_two,
        grad_out_bias,
        grad_up_bias,
        grad_down_bias,
    )
    return (
        final.reshape(set_count, tok_count, features),
        grad_input.reshape(set_count, tok_count, features),
        local_grads,
    )


def body(
    inputs,
    segment_ids,
    cotangent,
    qkv_weight,
    out_weight,
    up_weight,
    down_weight,
    first_gain,
    first_bias,
    second_gain,
    second_bias,
    out_bias,
    up_bias,
    down_bias,
):
    shards = (
        qkv_weight,
        out_weight,
        up_weight,
        down_weight,
        first_gain,
        first_bias,
        second_gain,
        second_bias,
        out_bias,
        up_bias,
        down_bias,
    )
    shard_sums = tuple((jnp.zeros(member.shape, jnp.float32) for member in shards))
    outcomes = []
    input_grads = []
    for micro_index in range(inputs.shape[0]):
        gathered = (
            lax.all_gather(qkv_weight, ("batch", "blk"), axis=0, tiled=True),
            lax.all_gather(out_weight, ("batch", "blk"), axis=0, tiled=True),
            lax.all_gather(up_weight, ("batch", "blk"), axis=0, tiled=True),
            lax.all_gather(down_weight, ("batch", "blk"), axis=0, tiled=True),
            lax.all_gather(first_gain, ("batch", "blk"), axis=0, tiled=True),
            lax.all_gather(first_bias, ("batch", "blk"), axis=0, tiled=True),
            lax.all_gather(second_gain, ("batch", "blk"), axis=0, tiled=True),
            lax.all_gather(second_bias, ("batch", "blk"), axis=0, tiled=True),
            lax.all_gather(out_bias, ("batch", "blk"), axis=0, tiled=True),
            lax.all_gather(up_bias, ("batch", "blk"), axis=0, tiled=True),
            lax.all_gather(down_bias, ("batch", "blk"), axis=0, tiled=True),
        )
        final, grad_input, local_grads = micro_step(
            inputs[micro_index], segment_ids[micro_index], cotangent[micro_index], gathered
        )
        outcomes.append(final)
        input_grads.append(grad_input)
        summed = (
            lax.psum_scatter(local_grads[0], ("batch", "blk"), scatter_dimension=0, tiled=True),
            lax.psum_scatter(local_grads[1], ("batch", "blk"), scatter_dimension=0, tiled=True),
            lax.psum_scatter(local_grads[2], ("batch", "blk"), scatter_dimension=0, tiled=True),
            lax.psum_scatter(local_grads[3], ("batch", "blk"), scatter_dimension=0, tiled=True),
            lax.psum_scatter(local_grads[4], ("batch", "blk"), scatter_dimension=0, tiled=True),
            lax.psum_scatter(local_grads[5], ("batch", "blk"), scatter_dimension=0, tiled=True),
            lax.psum_scatter(local_grads[6], ("batch", "blk"), scatter_dimension=0, tiled=True),
            lax.psum_scatter(local_grads[7], ("batch", "blk"), scatter_dimension=0, tiled=True),
            lax.psum_scatter(local_grads[8], ("batch", "blk"), scatter_dimension=0, tiled=True),
            lax.psum_scatter(local_grads[9], ("batch", "blk"), scatter_dimension=0, tiled=True),
            lax.psum_scatter(local_grads[10], ("batch", "blk"), scatter_dimension=0, tiled=True),
        )
        shard_sums = tuple((former + latter for former, latter in zip(shard_sums, summed)))
    return (jnp.stack(outcomes), jnp.stack(input_grads)) + tuple(shard_sums)


AXES = ("batch", "blk")
Y, C, ZH, Z0, X = 16, 8, 4, 2, 1
TEAM = (0, Z0, C, C | Z0)


def swap(values, mask):
    return lax.ppermute(values, AXES, [(i, i ^ mask) for i in range(32)])


def regroup(values, flip):
    pairs = []
    for i in range(32):
        core, right = (i >> 3) & 1, i & 1
        pairs.append((i, (i & (Y | Z0)) | (right << 3) | ((i & ZH) ^ (flip << 2)) | core))
    return lax.ppermute(values, AXES, pairs)


def ordered(near, far, bit, axis):
    return jnp.stack((jnp.where(bit == 0, near, far), jnp.where(bit == 0, far, near)), axis)


def grow(values, axis, bit, mask):
    return ordered(values, swap(values, mask), bit, axis)


def pick(values, place, axis=0):
    return lax.dynamic_index_in_dim(values, place, axis, keepdims=False)


def shrink(values, axis, bit, mask):
    got = swap(pick(values, 1 - bit, axis), mask)
    return pick(values, bit, axis).astype(jnp.float32) + got.astype(jnp.float32)


def tie(*values):
    return lax.optimization_barrier(values)


def low(values):
    return values.astype(jnp.bfloat16)


def wide(values):
    return values.astype(jnp.float32)


def team_trade(parts, quarter, bit_c, bit_z):
    own = pick(parts, quarter)
    got = [swap(pick(parts, quarter ^ r), TEAM[r]) for r in (1, 2, 3)]
    return ordered(
        ordered(own, got[0], bit_z, 0), ordered(got[1], got[2], bit_z, 0), bit_c, 0
    )


def team_gather(rows):
    near = jnp.concatenate((rows, swap(rows, Z0)), 0)
    return jnp.concatenate((near, swap(near, C)), 0)


def team_scatter(near, far):
    half = near.shape[0] // 2
    near = wide(near) + wide(swap(low(far), C))
    return near[:half] + wide(swap(low(near[half:]), Z0))


def dot_t(former, latter):
    return lax.dot_general(
        former, latter, (((1,), (1,)), ((), ())), preferred_element_type=jnp.float32
    )


def dot_rows(former, latter):
    return lax.dot_general(
        former, latter, (((0,), (0,)), ((), ())), preferred_element_type=jnp.float32
    )


STEP = 256
HEAD = 128


def image_of(ends, flips, shape, axis, base=0):
    row = lax.broadcasted_iota(jnp.int32, shape, axis) + base
    block = row >> 7
    chunk = 4 * ((block & 1) ^ flips[0]) + 2 * (((block >> 1) & 1) ^ flips[1])
    chunk = chunk + ((block >> 2) ^ flips[2])
    spot = (chunk * 128 + (row & 127)).astype(jnp.float32)
    return sum(jnp.where(spot >= ends[i], 1.0, 0.0) for i in range(3))


LOG2E = 1.4426950408889634


def attend_kernel(ends, flips, mixed, near, far, logs, images):
    rows = mixed.shape[0]
    heads = near.shape[1] // HEAD
    scale = HEAD ** (-0.5) * LOG2E
    images[...] = image_of(ends, flips, images.shape, 0)

    def block(number, unused):
        start = pl.multiple_of(number * STEP, STEP)
        spot = pl.ds(start, STEP)
        target = pl.ds(pl.multiple_of((number >> 1) * STEP, STEP), STEP)
        image = image_of(ends, flips, (1, STEP), 1, start)
        column = images[...]
        same = jnp.concatenate([column] * (STEP // HEAD), 1) == image

        def one_head(head, unused):
            at_q, at_k, at_v = (
                pl.ds(pl.multiple_of((part * heads + head) * HEAD, HEAD), HEAD) for part in range(3)
            )
            scores = dot_t(mixed[:, at_k], mixed[spot, at_q])
            scores = jnp.where(same, scores * scale, masked_score)
            highest = jnp.max(scores, axis=0, keepdims=True)
            shares = jnp.exp2(scores - highest)
            total = jnp.sum(shares, axis=0, keepdims=True)
            mixture = dot_rows(mixed[:, at_v], low(shares)) / total
            mixture = low(mixture.T)
            logs[pl.ds(head, 1), spot] = highest + jnp.log2(total)

            @pl.when(number % 2 == 0)
            def _():
                near[target, at_q] = mixture

            @pl.when(number % 2 == 1)
            def _():
                far[target, at_q] = mixture

            return unused

        return lax.fori_loop(0, heads, one_head, unused)

    lax.fori_loop(0, rows // STEP, block, 0)


def attend_back_kernel(
    ends, flips, mixed, near, far, logs, out, key_sum, value_sum, images, both
):
    rows = mixed.shape[0]
    heads = near.shape[1] // HEAD
    scale = HEAD ** (-0.5)
    images[...] = image_of(ends, flips, images.shape, 0)
    key_sum[...] = jnp.zeros_like(key_sum)
    value_sum[...] = jnp.zeros_like(value_sum)
    for number in range(rows // STEP):
        source = (near, far)[number % 2]
        spot = (number // 2) * STEP
        both[number * STEP : (number + 1) * STEP] = source[spot : spot + STEP]

    def block(number, unused):
        start = pl.multiple_of(number * STEP, STEP)
        spot = pl.ds(start, STEP)
        image = image_of(ends, flips, (1, STEP), 1, start)
        column = images[...]
        same = jnp.concatenate([column] * (STEP // HEAD), 1) == image

        def one_head(head, unused):
            at_q, at_k, at_v = (
                pl.ds(pl.multiple_of((part * heads + head) * HEAD, HEAD), HEAD) for part in range(3)
            )
            queries = mixed[spot, at_q]
            grad = both[spot, at_q]
            keys = mixed[:, at_k]
            scores = dot_t(keys, queries) * (scale * LOG2E) - logs[pl.ds(head, 1), spot]
            shares = jnp.exp2(jnp.where(same, scores, masked_score))
            grad_shares = dot_t(mixed[:, at_v], grad)
            delta = jnp.sum(shares * grad_shares, axis=0, keepdims=True)
            grad_scores = low(shares * (grad_shares - delta))
            value_sum[:, at_q] += jnp.dot(low(shares), grad, preferred_element_type=jnp.float32)
            key_sum[:, at_q] += jnp.dot(grad_scores, queries, preferred_element_type=jnp.float32)
            out[spot, at_q] = low((dot_rows(keys, grad_scores) * scale).T)
            return unused

        return lax.fori_loop(0, heads, one_head, unused)

    lax.fori_loop(0, rows // STEP, block, 0)
    width = heads * HEAD
    out[:, width : 2 * width] = low(key_sum[...] * scale)
    out[:, 2 * width :] = low(value_sum[...])


def in_smem():
    return pl.BlockSpec(memory_space=pltpu.SMEM)


def in_vmem():
    return pl.BlockSpec(memory_space=pltpu.VMEM)


def attend(ends, flips, mixed):
    rows, columns = mixed.shape
    heads = columns // (3 * HEAD)
    work = 2 * rows * rows * HEAD * heads
    half = jax.ShapeDtypeStruct((rows // 2, heads * HEAD), jnp.bfloat16)
    return pl.pallas_call(
        attend_kernel,
        in_specs=[in_smem(), in_smem(), in_vmem()],
        out_shape=(half, half, jax.ShapeDtypeStruct((heads, rows), jnp.float32)),
        scratch_shapes=[pltpu.VMEM((rows, HEAD), jnp.float32)],
        compiler_params=pltpu.CompilerParams(vmem_limit_bytes=16 << 20),
        cost_estimate=pl.CostEstimate(
            flops=18 * work, transcendentals=rows * rows * heads, bytes_accessed=4 << 20
        ),
        name="attend",
    )(ends, flips, mixed)


def attend_back(ends, flips, mixed, near, far, logs):
    rows, columns = mixed.shape
    heads = columns // (3 * HEAD)
    work = 2 * rows * rows * HEAD * heads
    return pl.pallas_call(
        attend_back_kernel,
        in_specs=[in_smem(), in_smem()] + [in_vmem()] * 4,
        out_shape=jax.ShapeDtypeStruct((rows, columns), jnp.bfloat16),
        scratch_shapes=[
            pltpu.VMEM((rows, heads * HEAD), jnp.float32),
            pltpu.VMEM((rows, heads * HEAD), jnp.float32),
            pltpu.VMEM((rows, HEAD), jnp.float32),
            pltpu.VMEM((rows, heads * HEAD), jnp.bfloat16),
        ],
        compiler_params=pltpu.CompilerParams(vmem_limit_bytes=20 << 20),
        cost_estimate=pl.CostEstimate(
            flops=22 * work, transcendentals=rows * rows * heads, bytes_accessed=6 << 20
        ),
        name="attend_back",
    )(ends, flips, mixed, near, far, logs)


def split_kernel(quarter, qkv, up, ids, up_vector, *refs):
    singles, outs, board = refs[:6], refs[6:10], refs[10]
    board[...] = jnp.zeros_like(board)
    for i, single in enumerate(singles):
        board[i : i + 1, :32] = wide(single[...])
    for i in range(4):
        board[6 + i : 7 + i, :32] = wide(up_vector[:, 32 * i : 32 * i + 32])
    for m in range(2):
        for i in range(3):
            below = jnp.where(ids[m : m + 1] <= i, 1.0, 0.0)
            below = jnp.sum(below, axis=1, keepdims=True)
            board[10 + 3 * m + i : 11 + 3 * m + i, :] = jnp.broadcast_to(below, (1, 128))
    extra = low(board[...].T[:32])
    for r, out in enumerate(outs):
        member = quarter[0] ^ r
        for part in range(6):
            spot = pl.ds(pl.multiple_of((4 * part + member) * HEAD, HEAD), HEAD)
            out[:, part * HEAD : (part + 1) * HEAD] = qkv[:, spot]
        out[:, 6 * HEAD : 7 * HEAD] = extra
        for part in range(8):
            block = 16 * (part >> 2) + 8 * (member >> 1) + 4 * ((part >> 1) & 1)
            block = block + 2 * (member & 1) + (part & 1)
            spot = pl.ds(pl.multiple_of(block * HEAD, HEAD), HEAD)
            out[:, (7 + part) * HEAD : (8 + part) * HEAD] = up[:, spot]


def split(quarter, qkv, up, ids, up_vector, singles):
    rows = qkv.shape[0]
    return pl.pallas_call(
        split_kernel,
        in_specs=[in_smem()] + [in_vmem()] * 10,
        out_shape=[jax.ShapeDtypeStruct((rows, 15 * HEAD), jnp.bfloat16)] * 4,
        out_specs=[in_vmem()] * 4,
        scratch_shapes=[pltpu.VMEM((128, 128), jnp.float32)],
        cost_estimate=pl.CostEstimate(flops=0, transcendentals=0, bytes_accessed=1 << 20),
        name="split",
    )(
        quarter.reshape(1),
        qkv,
        up,
        ids.reshape(2, -1),
        up_vector.reshape(1, -1),
        *(single.reshape(1, -1) for single in singles),
    )


def join_kernel(quarter, own, got_z, got_c, got_both, qkv, up):
    for r, part_of in enumerate((own, got_z, got_c, got_both)):
        member = quarter[0] ^ r
        for part in range(6):
            spot = pl.ds(pl.multiple_of((4 * part + member) * HEAD, HEAD), HEAD)
            qkv[:, spot] = wide(part_of[:, part * HEAD : (part + 1) * HEAD])
        for part in range(8):
            block = 16 * (part >> 2) + 8 * (member >> 1) + 4 * ((part >> 1) & 1)
            block = block + 2 * (member & 1) + (part & 1)
            spot = pl.ds(pl.multiple_of(block * HEAD, HEAD), HEAD)
            up[:, spot] = wide(part_of[:, (6 + part) * HEAD : (7 + part) * HEAD])


def join(quarter, parts):
    rows = parts[0].shape[0]
    return pl.pallas_call(
        join_kernel,
        in_specs=[in_smem()] + [in_vmem()] * 4,
        out_shape=[jax.ShapeDtypeStruct((rows, n * HEAD), jnp.float32) for n in (24, 32)],
        out_specs=[in_vmem()] * 2,
        cost_estimate=pl.CostEstimate(flops=0, transcendentals=0, bytes_accessed=8 << 20),
        name="join",
    )(quarter.reshape(1), *parts)


def outer_kernel(former_near, former_far, latter_near, latter_far, out):
    def block(number, unused):
        spot = pl.ds(pl.multiple_of(number * STEP, STEP), STEP)
        total = dot_rows(former_near[:, spot], latter_near[...])
        out[spot] = low(total + dot_rows(former_far[:, spot], latter_far[...]))
        return unused

    lax.fori_loop(0, out.shape[0] // STEP, block, 0)


def outer(former_near, former_far, latter_near, latter_far):
    count, rows = former_near.shape
    columns = latter_near.shape[1]
    return pl.pallas_call(
        outer_kernel,
        out_shape=jax.ShapeDtypeStruct((rows, columns), jnp.bfloat16),
        compiler_params=pltpu.CompilerParams(vmem_limit_bytes=20 << 20),
        cost_estimate=pl.CostEstimate(
            flops=6 * count * rows * columns, transcendentals=0, bytes_accessed=6 << 20
        ),
        name="outer",
    )(former_near, former_far, latter_near, latter_far)


def feed_kernel(rows, grads, w_up, w_down, bias, activ, grad_up, back, forth, sums):
    step = rows.shape[0]
    pieces = w_up.shape[1] // STEP
    sums[...] = jnp.zeros_like(sums)

    def places(number):
        spot = pl.ds(pl.multiple_of((number // pieces) * step, step), step)
        return spot, pl.ds(pl.multiple_of((number % pieces) * STEP, STEP), STEP)

    def inner(number, unused):
        spot, unit = places(number)
        upper = dense(rows[spot], w_up[:, unit]) + bias[:, unit]
        share = 0.5 + 0.5 * lax.erf(upper * (0.5**0.5))
        activ[spot, unit] = low(upper * share)
        slope = share + upper * jnp.exp(-0.5 * upper * upper) * 0.3989422804014327
        grad = low(dot_t(grads[spot], w_down[unit]) * slope)
        grad_up[spot, unit] = grad
        sums[:, unit] += jnp.sum(wide(grad), axis=0, keepdims=True)
        return unused

    def outwards(number, unused):
        spot, unit = places(number)
        back[spot, unit] = low(dot_t(grad_up[spot], w_up[unit]))
        forth[spot, unit] = low(dense(activ[spot], w_down[:, unit]))
        return unused

    count = (rows.shape[0] // step) * pieces
    lax.fori_loop(0, count, inner, 0)
    lax.fori_loop(0, count, outwards, 0)


def feed(rows, grads, w_up, w_down, bias):
    count, features = rows.shape
    hidden = w_up.shape[1]
    kind = jnp.bfloat16
    return pl.pallas_call(
        feed_kernel,
        out_shape=(
            jax.ShapeDtypeStruct((count, hidden), kind),
            jax.ShapeDtypeStruct((count, hidden), kind),
            jax.ShapeDtypeStruct((count, features), kind),
            jax.ShapeDtypeStruct((count, features), kind),
            jax.ShapeDtypeStruct((1, hidden), jnp.float32),
        ),
        compiler_params=pltpu.CompilerParams(vmem_limit_bytes=28 << 20),
        cost_estimate=pl.CostEstimate(
            flops=11 * count * features * hidden,
            transcendentals=2 * count * hidden,
            bytes_accessed=8 << 20,
        ),
        name="feed",
    )(rows, grads, w_up, w_down, bias)


def team_body(
    inputs,
    segment_ids,
    cotangent,
    qkv_weight,
    out_weight,
    up_weight,
    down_weight,
    first_gain,
    first_bias,
    second_gain,
    second_bias,
    out_bias,
    up_bias,
    down_bias,
):
    batch_at, blk_at = lax.axis_index("batch"), lax.axis_index("blk")
    y, c = batch_at >> 1, batch_at & 1
    zh, z0, x = blk_at >> 2, (blk_at >> 1) & 1, blk_at & 1
    quarter = 2 * c + z0
    tokens, features = inputs.shape[2:]

    def send_rows(values):
        return [regroup(pick(values[:, 0], zh ^ flip), flip) for flip in (0, 1)]

    rows_near, rows_far = send_rows(inputs)
    grad_near, grad_far = send_rows(cotangent)
    singles = (first_gain, first_bias, second_gain, second_bias, out_bias, down_bias)
    own, *others = split(quarter, qkv_weight, up_weight, segment_ids, up_bias, singles)
    got = [swap(other, mask) for other, mask in zip(others, TEAM[1:])]
    w_out = grow(out_weight, 0, zh, ZH)
    own, *got, w_out, down_weight, grad_near, grad_far = tie(
        own, *got, w_out, down_weight, grad_near, grad_far
    )

    parts = ordered(ordered(own, got[0], z0, 0), ordered(got[1], got[2], z0, 0), c, 0)
    w_qkv = grow(parts[..., :896], 1, zh, ZH)
    w_up = parts[..., 896:]
    rows = wide(jnp.concatenate((rows_near, rows_far), 0))
    average = jnp.mean(rows, axis=-1, keepdims=True)
    centred = rows - average
    inverse_one = lax.rsqrt(jnp.mean(centred * centred, axis=-1, keepdims=True) + epsilon)
    scaled_one = centred * inverse_one
    sent = low(scaled_one)
    side = jnp.concatenate((sent, swap(sent, Z0)), 0)
    across = swap(side, C)
    w_qkv, down_weight = tie(w_qkv, down_weight)
    w_near = grow(w_qkv[0], 2, x, X)
    w_far = grow(w_qkv[1], 0, y, Y)
    w_near = grow(w_near, 0, y, Y)
    w_far = grow(w_far, 3, x, X)
    w_down = grow(down_weight, 0, zh, ZH)
    w_out = grow(grow(w_out, 1, z0, Z0), 0, y, Y)
    side, across, w_near, w_far, w_out, w_up, w_down, grad_near, grad_far = tie(
        side, across, w_near, w_far, w_out, w_up, w_down, grad_near, grad_far
    )

    w_qkv = jnp.stack((w_near, w_far), 1).reshape(features, -1)
    extra = wide(w_qkv[:, 768:]).T
    w_qkv = w_qkv[:, :768]
    gain_one, shift_one, gain_two, shift_two, bias_out, bias_down = (
        extra[i : i + 1] for i in range(6)
    )
    bias_up = extra[6:10].reshape(4, 2, 2, 2, 2, 2, 32)
    bias_up = pick(pick(bias_up, z0, 4), c, 2).transpose(1, 2, 3, 0, 4).reshape(1, -1)
    place = jnp.arange(features)
    ours = ((place >> 9) == y) & (((place >> 8) & 1) == x)
    ends = jnp.where(ours[None], lax.dynamic_slice_in_dim(extra, 10 + 3 * zh, 3, 0), 0.0)
    ends = jnp.sum(ends, 1) * (1.0 / 32.0)
    flips = jnp.stack((zh, z0, c))
    normed = low(wide(jnp.concatenate((side, across), 0)) * gain_one + shift_one)
    grad_own = jnp.concatenate((grad_near, grad_far), 0)
    grad_side = jnp.concatenate((grad_own, swap(grad_own, Z0)), 0)
    out_got = swap(w_out, X)
    down_near, down_far = w_down[:, :64], w_down[:, 64:]
    near_got = swap(down_near, Y)
    far_got = swap(down_far, X)
    up_got = swap(w_up, ZH)
    mixed = low(dense(normed, w_qkv))
    attended, away, logs = attend(ends, flips, mixed)
    came = swap(away, Z0)
    attended, out_got, up_got, near_got, far_got, grad_side = tie(
        attended, out_got, up_got, near_got, far_got, grad_side
    )
    w_out = ordered(w_out, out_got, x, 3)
    down_near = ordered(down_near, near_got, y, 0)
    down_far = ordered(down_far, far_got, x, 1)
    w_up = ordered(w_up, up_got, zh, 1)

    tokens_two = 2 * tokens
    out_both = jnp.concatenate(
        [pick(w_out, place, 1).reshape(-1, features) for place in (z0, 1 - z0)], 0
    )
    grad_across = swap(grad_side, C)
    w_near = grow(w_up[0], 2, x, X)
    w_far = grow(w_up[1], 0, y, Y)
    came, out_both, grad_across, down_near, down_far = tie(
        came, out_both, grad_across, down_near, down_far
    )
    down_near = grow(down_near, 2, x, X)
    down_far = grow(down_far, 0, y, Y)

    both = jnp.concatenate((attended, came), 1)
    far = dense(both[tokens_two:], out_both)
    near = dense(both[:tokens_two], out_both)
    middle = rows + near + wide(swap(low(far), C)) + bias_out
    normed_two, scaled_two, inverse_two = norm_rows(middle, gain_two, shift_two)
    normed_two = low(normed_two)
    near = jnp.concatenate((normed_two, swap(normed_two, Z0)), 0)
    far = swap(near, C)
    w_near = grow(w_near, 0, y, Y)
    w_far = grow(w_far, 3, x, X)
    w_up = jnp.stack((w_near, w_far), 1).reshape(features, -1)
    w_down = jnp.stack((down_near, down_far), 3).reshape(-1, features)
    near, far, w_down, w_up, grad_side, grad_across = tie(
        near, far, w_down, w_up, grad_side, grad_across
    )

    activ_far, upper_far, back_far, forth_far, sums_far = feed(
        far, grad_across, w_up, w_down, bias_up
    )
    activ, upper, back, forth, sums_near = feed(near, grad_side, w_up, w_down, bias_up)
    back, forth, back_far, forth_far, activ, upper = tie(
        back, forth, swap(back_far, C), swap(forth_far, C), activ, upper
    )

    count = back.shape[0] // 2
    back_own = wide(back[:count]) + wide(back_far[:count])
    back_other = low(wide(back[count:]) + wide(back_far[count:]))
    grad_two = back_own + wide(swap(back_other, Z0))
    grad_down = outer(activ, activ_far, grad_side, grad_across).reshape(2, 2, 2, 128, features)
    grad_up = outer(near, far, upper, upper_far).reshape(2, 2, 2, 2, 2, 32, -1)
    down_got = swap(pick(grad_down, 1 - y), Y)
    up_got = swap(pick(grad_up, 1 - x, 4), X)
    grad_two, grad_down, grad_up, forth, forth_far = tie(
        grad_two, grad_down, grad_up, forth, forth_far
    )

    grad_middle = wide(grad_own) + norm_back(grad_two, scaled_two, inverse_two, gain_two)
    branch_own = low(grad_middle)
    branch_own, branch, forth, forth_far = tie(
        branch_own, swap(branch_own, C), forth, forth_far
    )
    branch = jnp.concatenate((branch_own, branch), 0)
    grad_both = low(dot_t(branch, out_both))
    width = attended.shape[1]
    grad_attended = grad_both[:, :width]
    grad_came = swap(grad_both[:, width:], Z0)
    grad_w_out = low(dot_rows(both, branch)).reshape(2, 2, 2, 2, 32, features)
    grad_w_out = ordered(grad_w_out[0], grad_w_out[1], z0, 1)
    forth_own = wide(forth[:count]) + wide(forth_far[:count])
    forth_other = low(wide(forth[count:]) + wide(forth_far[count:]))
    final = low(middle + forth_own + wide(swap(forth_other, Z0)) + bias_down)
    grad_came, down_got, up_got, grad_w_out, final = tie(
        grad_came, down_got, up_got, grad_w_out, final
    )
    grad_down = low(wide(pick(grad_down, y)) + wide(down_got))
    grad_up = low(wide(pick(grad_up, x, 4)) + wide(up_got))

    def give_rows(values):
        got = (regroup(values[:tokens], 0), regroup(values[tokens:], 1))
        return wide(ordered(*got, zh, 0))[:, None]

    grad_down = low(shrink(grad_down, 1, x, X))
    grad_up = low(shrink(grad_up, 0, y, Y))
    grad_mixed = attend_back(ends, flips, mixed, grad_attended, grad_came, logs)
    final = give_rows(final)
    grad_w_out = low(shrink(grad_w_out, 0, y, Y))
    grad_mixed, grad_up, grad_down, final = tie(grad_mixed, grad_up, grad_down, final)

    half = 2 * tokens_two
    far = swap(low(dot_t(grad_mixed[half:], w_qkv)), C)
    back = dot_t(grad_mixed[:half], w_qkv)
    grad_qkv = low(dot_rows(normed, grad_mixed)).reshape(2, 2, 2, 2, 2, 32, -1)
    far, back, grad_qkv, grad_w_out, grad_up, grad_down = tie(
        far, back, grad_qkv, grad_w_out, grad_up, grad_down
    )
    back = back + wide(far)
    grad_one = back[:count] + wide(swap(low(back[count:]), Z0))
    qkv_near = low(shrink(low(shrink(grad_qkv[:, 0], 3, x, X)), 0, y, Y))
    qkv_far = low(shrink(low(shrink(grad_qkv[:, 1], 0, y, Y)), 2, x, X))
    grads = jnp.stack((grad_down, grad_up.transpose(1, 0, 2, 3, 4).reshape(2, 128, -1)), 1)
    grads = shrink(grads, 0, zh, ZH)
    grad_down = grads[0]
    grad_up = low(grads[1]).reshape(4, 32, -1)
    grad_w_out = low(shrink(grad_w_out, 2, x, X))
    grad_qkv = jnp.stack((qkv_near, qkv_far), 0)
    given = low(grad_middle + norm_back(grad_one, scaled_one, inverse_one, gain_one))
    given, grad_qkv, grad_w_out, grad_up, grad_down, grad_one = tie(
        given, grad_qkv, grad_w_out, grad_up, grad_down, grad_one
    )

    input_grad = give_rows(given)
    qkv_got = swap(pick(grad_qkv, 1 - zh, 1), ZH)
    out_got = swap(pick(grad_w_out, 1 - zh), ZH)
    qkv_got, out_got, grad_one = tie(qkv_got, out_got, grad_one)
    grad_qkv = low(wide(pick(grad_qkv, zh, 1)) + wide(qkv_got)).reshape(4, 32, -1)
    grad_w_out = wide(pick(grad_w_out, zh)) + wide(out_got)
    parts = jnp.concatenate((grad_qkv, grad_up), 2)
    parts = [pick(parts, quarter ^ r) for r in range(4)]
    parts[1] = jnp.concatenate((parts[1], low(pick(grad_w_out, 1 - z0))), 1)
    parts = parts[:1] + [swap(part, mask) for part, mask in zip(parts[1:], TEAM[1:])]
    grad_w_out = pick(grad_w_out, z0) + wide(parts[1][:, 1792:])
    grad_qkv, grad_up = join(quarter, parts)
    sums = jnp.stack(
        (
            jnp.sum(grad_one * scaled_one, 0),
            jnp.sum(grad_one, 0),
            jnp.sum(grad_two * scaled_two, 0),
            jnp.sum(grad_two, 0),
            jnp.sum(wide(branch_own), 0),
            jnp.sum(wide(grad_own), 0),
        )
    )
    sums = sums.reshape(6, 32, 32).transpose(1, 0, 2).reshape(32, 192)
    up_sums = (sums_near + sums_far).reshape(8, 1, 128)
    up_sums = jnp.where(jnp.arange(4)[None, :, None] == quarter, up_sums, 0.0)
    up_sums = up_sums.reshape(2, 2, 2, 2, 2, 128).transpose(0, 3, 1, 4, 2, 5).reshape(32, 128)
    sums = jnp.concatenate((up_sums, sums), 1)
    sums = jnp.sum(lax.all_to_all(sums, AXES, 0, 0, tiled=True), 0)
    grad_up_bias = sums[:128]
    small = [sums[128 + 32 * i : 160 + 32 * i] for i in range(6)]
    return (
        final,
        input_grad,
        grad_qkv,
        grad_w_out,
        grad_up,
        grad_down,
        small[0],
        small[1],
        small[2],
        small[3],
        small[4],
        grad_up_bias,
        small[5],
    )


def chosen_body(mesh, *arrays):
    shape = arrays[0].shape
    sizes = (mesh.shape["batch"], mesh.shape["blk"])
    if sizes == (4, 8) and shape == (2, 1, 128, 1024) and arrays[5].shape == (32, 4096):
        return team_body(*arrays)
    return body(*arrays)


def solution(mesh):
    return jax.shard_map(
        partial(chosen_body, mesh),
        mesh=mesh,
        in_specs=(
            P(None, "batch", "blk", None),
            P(None, "batch", "blk"),
            P(None, "batch", "blk", None),
            P(("batch", "blk"), None),
            P(("batch", "blk"), None),
            P(("batch", "blk"), None),
            P(("batch", "blk"), None),
            P(("batch", "blk")),
            P(("batch", "blk")),
            P(("batch", "blk")),
            P(("batch", "blk")),
            P(("batch", "blk")),
            P(("batch", "blk")),
            P(("batch", "blk")),
        ),
        out_specs=(
            P(None, "batch", "blk", None),
            P(None, "batch", "blk", None),
            P(("batch", "blk"), None),
            P(("batch", "blk"), None),
            P(("batch", "blk"), None),
            P(("batch", "blk"), None),
            P(("batch", "blk")),
            P(("batch", "blk")),
            P(("batch", "blk")),
            P(("batch", "blk")),
            P(("batch", "blk")),
            P(("batch", "blk")),
            P(("batch", "blk")),
        ),
        check_vma=False,
    )
```

profile of v0, /device:TPU:0, one launch (start us, length us, event | category | flops | bytes accessed | tf_op | source)
XLA Modules:
  0.0 297.8 jit_solution(81938102783023705)
XLA Ops:
  2.5 4.1 %collective-permute-start.9 = (bf16[128,1024]{1,0:T(8,128)(2,1)S(1)}, bf16[128,1024]{1,0:T(8,128)(2,1)S(1)}, u32[]{:S(2)}, u32[]{:S(2)}) collective-permute-start(bf16[128,1024]{1,0:T(8,128)(2,1)S(1)} %get-tuple-element.273), channel_id=1, source_target_pairs={{0,4},{1,12},{2,6},{3,14},{4,0},{5,8},{6,2},{7,10},{8,5},{9,13},{1... | collective-permute-start | bytes 786440 | tf_op jit(solution)/shard_map/ppermute | solution.py:359
  13.7 7.0 %collective-permute-done.7 = bf16[32,1024]{1,0:T(8,128)(2,1)S(1)} collective-permute-done((bf16[32,1024]{1,0:T(8,128)(2,1)}, bf16[32,1024]{1,0:T(8,128)(2,1)S(1)}, u32[]{:S(2)}, u32[]{:S(2)}) %collective-permute-start.7) | collective-permute-done | bytes 65568 | tf_op jit(solution)/shard_map/ppermute | solution.py:351
  20.6 2.4 collective-permute-start.6
  23.7 3.2 %collective-permute-start.1 = (bf16[128,1024]{1,0:T(8,128)(2,1)S(1)}, bf16[128,1024]{1,0:T(8,128)(2,1)S(1)}, u32[]{:S(2)}, u32[]{:S(2)}) collective-permute-start(bf16[128,1024]{1,0:T(8,128)(2,1)S(1)} %get-tuple-element.276), channel_id=1, source_target_pairs={{0,4},{1,12},{2,6},{3,14},{4,0},{5,8},{6,2},{7,10},{8,5},{9,13},{1... | collective-permute-start | bytes 786440 | tf_op jit(solution)/shard_map/ppermute | solution.py:359
  28.0 4.2 %collective-permute-start.10 = (bf16[2,2,32,896]{3,2,1,0:T(8,128)(2,1)S(1)}, bf16[2,2,32,896]{3,2,1,0:T(8,128)(2,1)S(1)}, u32[]{:S(2)}, u32[]{:S(2)}) collective-permute-start(bf16[2,2,32,896]{3,2,1,0:T(8,128)(2,1)S(1)} %pad_maximum_fusion.26), channel_id=1, source_target_pairs={{0,4},{1,5},{2,6},{3,7},{4,0},{5,1},{6,2},{7,3},{8,12},{9,13},{10,... | collective-permute-start | bytes 688136 | tf_op jit(solution)/shard_map/ppermute | solution.py:351
  34.3 9.0 %collective-permute-done.1 = bf16[128,1024]{1,0:T(8,128)(2,1)S(1)} collective-permute-done((bf16[128,1024]{1,0:T(8,128)(2,1)S(1)}, bf16[128,1024]{1,0:T(8,128)(2,1)S(1)}, u32[]{:S(2)}, u32[]{:S(2)}) %collective-permute-start.1) | collective-permute-done | bytes 262176 | tf_op jit(solution)/shard_map/ppermute | solution.py:359
  45.8 2.5 collective-permute-done.10
  50.2 3.9 %collective-permute-start.11 = (bf16[2,2,32,896]{3,2,1,0:T(8,128)(2,1)S(1)}, bf16[2,2,32,896]{3,2,1,0:T(8,128)(2,1)S(1)}, u32[]{:S(2)}, u32[]{:S(2)}) collective-permute-start(bf16[2,2,32,896]{3,2,1,0:T(8,128)(2,1)S(1)} %slice_bitcast_fusion.1), channel_id=1, source_target_pairs={{0,1},{1,0},{2,3},{3,2},{4,5},{5,4},{6,7},{7,6},{8,9},{9,8},{10,11... | collective-permute-start | bytes 688136 | tf_op jit(solution)/shard_map/ppermute | solution.py:351
  54.2 3.8 %collective-permute-done.13 = bf16[2,2,32,896]{3,2,1,0:T(8,128)(2,1)S(1)} collective-permute-done((bf16[2,2,32,896]{3,2,1,0:T(8,128)(2,1)S(1)}, bf16[2,2,32,896]{3,2,1,0:T(8,128)(2,1)S(1)}, u32[]{:S(2)}, u32[]{:S(2)}) %collective-permute-start.13) | collective-permute-done | bytes 229408 | tf_op jit(solution)/shard_map/ppermute | solution.py:351
  61.0 5.3 %collective-permute-done.2 = bf16[256,1024]{1,0:T(8,128)(2,1)S(1)} collective-permute-done((bf16[256,1024]{1,0:T(8,128)(2,1)S(1)}, bf16[256,1024]{1,0:T(8,128)(2,1)S(1)}, u32[]{:S(2)}, u32[]{:S(2)}) %collective-permute-start.2) | collective-permute-done | bytes 524320 | tf_op jit(solution)/shard_map/ppermute | solution.py:351
  66.8 4.3 %collective-permute-done.14 = bf16[2,2,2,32,896]{4,3,2,1,0:T(8,128)(2,1)S(1)} collective-permute-done((bf16[2,2,2,32,896]{4,3,2,1,0:T(8,128)(2,1)S(1)}, bf16[2,2,2,32,896]{4,3,2,1,0:T(8,128)(2,1)S(1)}, u32[]{:S(2)}, u32[]{:S(2)}) %collective-permute-start.14) | collective-permute-done | bytes 458784 | tf_op jit(solution)/shard_map/ppermute | solution.py:351
  71.7 2.8 collective-permute-start.22
  84.1 8.5 %attend.1 = (bf16[512,256]{1,0:T(8,128)(2,1)S(1)}, bf16[512,256]{1,0:T(8,128)(2,1)S(1)}, f32[2,1024]{1,0:T(2,128)S(1)}) custom-call(f32[3]{0:T(128)S(1)} %broadcast_multiply_fusion.6.ends, s32[3]{0:T(128)S(1)} %pad_add_fusion.flips, bf16[1024,768]{1,0:T(8,128)(2,1)S(1)} %convolution_convert_fusion.1.mixed), custom_call_target="tpu_custom_call" | custom-call | flops 9663676416 | bytes 4194304 | tf_op jit(solution)/shard_map/attend/pallas_call | solution.py:539
  108.1 10.0 %collective-permute-done.31 = bf16[2,2,2,32,1024]{4,3,1,0,2:T(8,128)(2,1)S(1)} collective-permute-done((bf16[2,2,2,32,1024]{4,3,1,0,2:T(8,128)(2,1)S(1)}, bf16[2,2,2,32,1024]{4,3,1,0,2:T(8,128)(2,1)S(1)}, u32[]{:S(2)}, u32[]{:S(2)}) %collective-permute-start.31) | collective-permute-done | bytes 524320 | tf_op jit(solution)/shard_map/ppermute | solution.py:351
  124.4 7.2 %collective-permute-done.26 = bf16[256,1024]{1,0:T(8,128)(2,1)S(1)} collective-permute-done((bf16[256,1024]{1,0:T(8,128)(2,1)S(1)}, bf16[256,1024]{1,0:T(8,128)(2,1)S(1)}, u32[]{:S(2)}, u32[]{:S(2)}) %collective-permute-start.26) | collective-permute-done | bytes 524320 | tf_op jit(solution)/shard_map/ppermute | solution.py:351
  132.2 2.2 collective-permute-done.28
  136.7 6.7 %feed.3 = (bf16[512,1024]{1,0:T(8,128)(2,1)S(1)}, bf16[512,1024]{1,0:T(8,128)(2,1)S(1)}, bf16[512,1024]{1,0:T(8,128)(2,1)S(1)}, bf16[512,1024]{1,0:T(8,128)(2,1)S(1)}, f32[1,1024]{1,0:T(1,128)S(1)}) custom-call(bf16[512,1024]{1,0:T(8,128)(2,1)S(1)} %collective-permute-done.27.rows.former_far, bf16[512,1024]{1,0:T(8,128)(2,1)S(1)} %collective-permute-done.24.grads.latter_far, ...), custom_call_target="tpu_custom_call" | custom-call | flops 5905580032 | bytes 8388608 | tf_op jit(solution)/shard_map/feed/pallas_call | solution.py:704
  144.0 6.7 %feed.2 = (bf16[512,1024]{1,0:T(8,128)(2,1)S(1)}, bf16[512,1024]{1,0:T(8,128)(2,1)S(1)}, bf16[512,1024]{1,0:T(8,128)(2,1)S(1)}, bf16[512,1024]{1,0:T(8,128)(2,1)S(1)}, f32[1,1024]{1,0:T(1,128)S(1)}) custom-call(bf16[512,1024]{1,0:T(8,128)(2,1)S(1)} %pad_maximum_fusion.6.rows.former_near, bf16[512,1024]{1,0:T(8,128)(2,1)S(1)} %pad_maximum_fusion.4.grads.latter_near, ...), custom_call_target="tpu_custom_call" | custom-call | flops 5905580032 | bytes 8388608 | tf_op jit(solution)/shard_map/feed/pallas_call | solution.py:704
  151.4 3.0 %outer.3 = bf16[1024,1024]{1,0:T(8,128)(2,1)S(1)} custom-call(bf16[512,1024]{1,0:T(8,128)(2,1)S(1)} %pad_maximum_fusion.6.rows.former_near, bf16[512,1024]{1,0:T(8,128)(2,1)S(1)} %collective-permute-done.27.rows.former_far, bf16[512,1024]{1,0:T(8,128)(2,1)S(1)} %get-tuple-element.159.latter_near, bf16[512,1024]{1,0:T(8,128)(2,1)S(1)} %get-tuple-element.160.latter_far), custom_call_target="tpu_custom_call" | custom-call | flops 3221225472 | bytes 6291456 | tf_op jit(solution)/shard_map/outer/pallas_call | solution.py:658
  154.4 3.2 %outer.2 = bf16[1024,1024]{1,0:T(8,128)(2,1)S(1)} custom-call(bf16[512,1024]{1,0:T(8,128)(2,1)S(1)} %get-tuple-element.157.former_near, bf16[512,1024]{1,0:T(8,128)(2,1)S(1)} %get-tuple-element.158.former_far, bf16[512,1024]{1,0:T(8,128)(2,1)S(1)} %pad_maximum_fusion.4.grads.latter_near, bf16[512,1024]{1,0:T(8,128)(2,1)S(1)} %collective-permute-done.24.grads.latter_far), custom_call_target="tpu_custom_call" | custom-call | flops 3221225472 | bytes 6291456 | tf_op jit(solution)/shard_map/outer/pallas_call | solution.py:658
  157.6 7.2 %collective-permute-done.36 = bf16[256,1024]{1,0:T(8,128)(2,1)S(1)} collective-permute-done((bf16[256,1024]{1,0:T(8,128)(2,1)S(1)}, bf16[256,1024]{1,0:T(8,128)(2,1)S(1)}, u32[]{:S(2)}, u32[]{:S(2)}) %collective-permute-start.36) | collective-permute-done | bytes 524320 | tf_op jit(solution)/shard_map/ppermute | solution.py:351
  183.0 9.8 %collective-permute-done.41 = bf16[256,1024]{1,0:T(8,128)(2,1)} collective-permute-done((bf16[256,1024]{1,0:T(8,128)(2,1)}, bf16[256,1024]{1,0:T(8,128)(2,1)}, u32[]{:S(2)}, u32[]{:S(2)}) %collective-permute-start.41) | collective-permute-done | bytes 524320 | tf_op jit(solution)/shard_map/ppermute | solution.py:351
  202.6 3.5 %collective-permute-start.43 = (bf16[2,128,1024]{2,1,0:T(8,128)(2,1)S(1)}, bf16[2,128,1024]{2,1,0:T(8,128)(2,1)S(1)}, u32[]{:S(2)}, u32[]{:S(2)}) collective-permute-start(bf16[2,128,1024]{2,1,0:T(8,128)(2,1)S(1)} %dynamic-slice_bitcast_fusion.2), channel_id=1, source_target_pairs={{0,1},{1,0},{2,3},{3,2},{4,5},{5,4},{6,7},{7,6},{8,9},{9,8},{10,11... | collective-permute-start | bytes 1572872 | tf_op jit(solution)/shard_map/ppermute | solution.py:351
  209.2 10.6 %attend_back.1 = bf16[1024,768]{1,0:T(8,128)(2,1)S(1)} custom-call(f32[3]{0:T(128)S(1)} %broadcast_multiply_fusion.6.ends, s32[3]{0:T(128)S(1)} %pad_add_fusion.flips, bf16[1024,768]{1,0:T(8,128)(2,1)S(1)} %copy-done.4, bf16[512,256]{1,0:T(8,128)(2,1)S(1)} %get-tuple-element.256.near, bf16[512,256]{1,0:T(8,128)(2,1)} %collective-permute-done.38.far, ...), custom_call_target="tpu_custom_call" | custom-call | flops 11811160064 | bytes 6291456 | tf_op jit(solution)/shard_map/attend_back/pallas_call | solution.py:556
  234.3 4.3 %collective-permute-done.53 = bf16[2,2,32,1024]{3,2,1,0:T(8,128)(2,1)S(1)} collective-permute-done((bf16[2,2,32,1024]{3,2,1,0:T(8,128)(2,1)S(1)}, bf16[2,2,32,1024]{3,2,1,0:T(8,128)(2,1)S(1)}, u32[]{:S(2)}, u32[]{:S(2)}) %collective-permute-start.53) | collective-permute-done | bytes 262176 | tf_op jit(solution)/shard_map/ppermute | solution.py:351
  238.7 7.6 %collective-permute-done.49 = bf16[2,2,2,32,768]{4,3,2,1,0:T(8,128)(2,1)S(1)} collective-permute-done((bf16[2,2,2,32,768]{4,3,2,1,0:T(8,128)(2,1)S(1)}, bf16[2,2,2,32,768]{4,3,2,1,0:T(8,128)(2,1)S(1)}, u32[]{:S(2)}, u32[]{:S(2)}) %collective-permute-start.49) | collective-permute-done | bytes 393248 | tf_op jit(solution)/shard_map/ppermute | solution.py:351
  248.3 5.9 %collective-permute-done.54 = bf16[2,128,1024]{2,1,0:T(8,128)(2,1)S(1)} collective-permute-done((bf16[2,128,1024]{2,1,0:T(8,128)(2,1)S(1)}, bf16[2,128,1024]{2,1,0:T(8,128)(2,1)S(1)}, u32[]{:S(2)}, u32[]{:S(2)}) %collective-permute-start.54) | collective-permute-done | bytes 524320 | tf_op jit(solution)/shard_map/ppermute | solution.py:351
  254.4 2.9 collective-permute-done.48
  259.4 3.0 collective-permute-start.58
  263.2 17.1 %collective-permute-done.58 = bf16[2,32,1024]{2,1,0:T(8,128)(2,1)S(1)} collective-permute-done((bf16[2,32,1024]{2,1,0:T(8,128)(2,1)S(1)}, bf16[2,32,1024]{2,1,0:T(8,128)(2,1)S(1)}, u32[]{:S(2)}, u32[]{:S(2)}) %collective-permute-start.58) | collective-permute-done | bytes 131104 | tf_op jit(solution)/shard_map/ppermute | solution.py:351
  281.6 3.3 %all-to-all-start = ((f32[32,1,320]{2,1,0:T(1,128)}), f32[32,1,320]{2,1,0:T(1,128)S(1)}, u32[]{:S(2)}, u32[]{:S(2)}) async-start(f32[32,1,320]{2,1,0:T(1,128)} %copy.94), calls=%async_computation | async-start | bytes 98304 | tf_op jit(solution)/shard_map/all_to_all | solution.py:942
  289.1 3.1 %all-to-all-done = f32[32,1,320]{2,1,0:T(1,128)S(1)} async-done(((f32[32,1,320]{2,1,0:T(1,128)}), f32[32,1,320]{2,1,0:T(1,128)S(1)}, u32[]{:S(2)}, u32[]{:S(2)}) %all-to-all-start) | async-done | bytes 40992 | tf_op jit(solution)/shard_map/all_to_all | solution.py:942
  (338 shorter events, 117.3 us)
Async XLA Ops:
  1.8 25.2 %collective-permute-start.8 = (bf16[128,1024]{1,0:T(8,128)(2,1)S(1)}, bf16[128,1024]{1,0:T(8,128)(2,1)S(1)}, u32[]{:S(2)}, u32[]{:S(2)}) collective-permute-start(bf16[128,1024]{1,0:T(8,128)(2,1)S(1)} %get-tuple-element.274), channel_id=1, source_target_pairs={{0,0},{1,8},{2,2},{3,10},{4,4},{5,12},{6,6},{7,14},{8,1},{9,9},{10... | collective-permute-start | bytes 786440 | tf_op jit(solution)/shard_map/ppermute | solution.py:359
  2.5 24.5 %collective-permute-start.9 = (bf16[128,1024]{1,0:T(8,128)(2,1)S(1)}, bf16[128,1024]{1,0:T(8,128)(2,1)S(1)}, u32[]{:S(2)}, u32[]{:S(2)}) collective-permute-start(bf16[128,1024]{1,0:T(8,128)(2,1)S(1)} %get-tuple-element.273), channel_id=1, source_target_pairs={{0,4},{1,12},{2,6},{3,14},{4,0},{5,8},{6,2},{7,10},{8,5},{9,13},{1... | collective-permute-start | bytes 786440 | tf_op jit(solution)/shard_map/ppermute | solution.py:359
  6.6 14.1 %collective-permute-start.7 = (bf16[32,1024]{1,0:T(8,128)(2,1)}, bf16[32,1024]{1,0:T(8,128)(2,1)S(1)}, u32[]{:S(2)}, u32[]{:S(2)}) collective-permute-start(bf16[32,1024]{1,0:T(8,128)(2,1)} %param.18), channel_id=1, source_target_pairs={{0,4},{1,5},{2,6},{3,7},{4,0},{5,1},{6,2},{7,3},{8,12},{9,13},{10,... | collective-permute-start | bytes 196616 | tf_op jit(solution)/shard_map/ppermute | solution.py:351
  8.6 14.4 %collective-permute-start.4 = (bf16[32,1920]{1,0:T(8,128)(2,1)}, bf16[32,1920]{1,0:T(8,128)(2,1)S(1)}, u32[]{:S(2)}, u32[]{:S(2)}) collective-permute-start(bf16[32,1920]{1,0:T(8,128)(2,1)} %get-tuple-element.108), channel_id=1, source_target_pairs={{0,2},{1,3},{2,0},{3,1},{4,6},{5,7},{6,4},{7,5},{8,10},{9,11},{10,... | collective-permute-start | bytes 368648 | tf_op jit(solution)/shard_map/ppermute | solution.py:351
  23.7 19.6 %collective-permute-start.1 = (bf16[128,1024]{1,0:T(8,128)(2,1)S(1)}, bf16[128,1024]{1,0:T(8,128)(2,1)S(1)}, u32[]{:S(2)}, u32[]{:S(2)}) collective-permute-start(bf16[128,1024]{1,0:T(8,128)(2,1)S(1)} %get-tuple-element.276), channel_id=1, source_target_pairs={{0,4},{1,12},{2,6},{3,14},{4,0},{5,8},{6,2},{7,10},{8,5},{9,13},{1... | collective-permute-start | bytes 786440 | tf_op jit(solution)/shard_map/ppermute | solution.py:359
  28.0 20.3 %collective-permute-start.10 = (bf16[2,2,32,896]{3,2,1,0:T(8,128)(2,1)S(1)}, bf16[2,2,32,896]{3,2,1,0:T(8,128)(2,1)S(1)}, u32[]{:S(2)}, u32[]{:S(2)}) collective-permute-start(bf16[2,2,32,896]{3,2,1,0:T(8,128)(2,1)S(1)} %pad_maximum_fusion.26), channel_id=1, source_target_pairs={{0,4},{1,5},{2,6},{3,7},{4,0},{5,1},{6,2},{7,3},{8,12},{9,13},{10,... | collective-permute-start | bytes 688136 | tf_op jit(solution)/shard_map/ppermute | solution.py:351
  44.1 22.3 %collective-permute-start.2 = (bf16[256,1024]{1,0:T(8,128)(2,1)S(1)}, bf16[256,1024]{1,0:T(8,128)(2,1)S(1)}, u32[]{:S(2)}, u32[]{:S(2)}) collective-permute-start(bf16[256,1024]{1,0:T(8,128)(2,1)S(1)} %fusion.9), channel_id=1, source_target_pairs={{0,2},{1,3},{2,0},{3,1},{4,6},{5,7},{6,4},{7,5},{8,10},{9,11},{10,... | collective-permute-start | bytes 1572872 | tf_op jit(solution)/shard_map/ppermute | solution.py:351
  48.4 18.2 %collective-permute-start.17 = (bf16[128,1024]{1,0:T(8,128)(2,1)S(1)}, bf16[128,1024]{1,0:T(8,128)(2,1)S(1)}, u32[]{:S(2)}, u32[]{:S(2)}) collective-permute-start(bf16[128,1024]{1,0:T(8,128)(2,1)S(1)} %copy-done.25), channel_id=1, source_target_pairs={{0,4},{1,5},{2,6},{3,7},{4,0},{5,1},{6,2},{7,3},{8,12},{9,13},{10,... | collective-permute-start | bytes 786440 | tf_op jit(solution)/shard_map/ppermute | solution.py:351
  71.7 22.9 %collective-permute-start.22 = (bf16[256,1024]{1,0:T(8,128)(2,1)S(1)}, bf16[256,1024]{1,0:T(8,128)(2,1)}, u32[]{:S(2)}, u32[]{:S(2)}) collective-permute-start(bf16[256,1024]{1,0:T(8,128)(2,1)S(1)} %constant_dynamic-update-slice_fusion), channel_id=1, source_target_pairs={{0,2},{1,3},{2,0},{3,1},{4,6},{5,7},{6,4},{7,5},{8,10},{9,11},{10,... | collective-permute-start | bytes 1572872 | tf_op jit(solution)/shard_map/ppermute | solution.py:351
  77.7 19.7 %collective-permute-start.20 = (bf16[2,64,1024]{2,1,0:T(8,128)(2,1)}, bf16[2,64,1024]{2,1,0:T(8,128)(2,1)}, u32[]{:S(2)}, u32[]{:S(2)}) collective-permute-start(bf16[2,64,1024]{2,1,0:T(8,128)(2,1)} %get-tuple-element.268), channel_id=1, source_target_pairs={{0,16},{1,17},{2,18},{3,19},{4,20},{5,21},{6,22},{7,23},{8,24},{9,... | collective-permute-start | bytes 786440 | tf_op jit(solution)/shard_map/ppermute | solution.py:351
  78.5 18.9 %collective-permute-start.21 = (bf16[2,64,1024]{2,1,0:T(8,128)(2,1)}, bf16[2,64,1024]{2,1,0:T(8,128)(2,1)}, u32[]{:S(2)}, u32[]{:S(2)}) collective-permute-start(bf16[2,64,1024]{2,1,0:T(8,128)(2,1)} %get-tuple-element.267), channel_id=1, source_target_pairs={{0,1},{1,0},{2,3},{3,2},{4,5},{5,4},{6,7},{7,6},{8,9},{9,8},{10,11... | collective-permute-start | bytes 786440 | tf_op jit(solution)/shard_map/ppermute | solution.py:351
  80.2 17.2 %collective-permute-start.18 = (bf16[2,2,2,32,1024]{4,3,2,1,0:T(8,128)(2,1)S(1)}, bf16[2,2,2,32,1024]{4,3,2,1,0:T(8,128)(2,1)}, u32[]{:S(2)}, u32[]{:S(2)}) collective-permute-start(bf16[2,2,2,32,1024]{4,3,2,1,0:T(8,128)(2,1)S(1)} %pad_maximum_fusion.11), channel_id=1, source_target_pairs={{0,1},{1,0},{2,3},{3,2},{4,5},{5,4},{6,7},{7,6},{8,9},{9,8},{10,11... | collective-permute-start | bytes 1572872 | tf_op jit(solution)/shard_map/ppermute | solution.py:351
  80.6 16.9 %collective-permute-start.19 = (bf16[2,2,32,1024]{3,2,1,0:T(8,128)(2,1)S(1)}, bf16[2,2,32,1024]{3,2,1,0:T(8,128)(2,1)}, u32[]{:S(2)}, u32[]{:S(2)}) collective-permute-start(bf16[2,2,32,1024]{3,2,1,0:T(8,128)(2,1)S(1)} %pad_maximum_fusion.22), channel_id=1, source_target_pairs={{0,4},{1,5},{2,6},{3,7},{4,0},{5,1},{6,2},{7,3},{8,12},{9,13},{10,... | collective-permute-start | bytes 786440 | tf_op jit(solution)/shard_map/ppermute | solution.py:351
  106.8 13.9 %collective-permute-start.33 = (bf16[2,2,2,32,1024]{4,3,2,1,0:T(8,128)(2,1)S(1)}, bf16[2,2,2,32,1024]{4,3,2,1,0:T(8,128)(2,1)S(1)}, u32[]{:S(2)}, u32[]{:S(2)}) collective-permute-start(bf16[2,2,2,32,1024]{4,3,2,1,0:T(8,128)(2,1)S(1)} %pad_maximum_fusion.16), channel_id=1, source_target_pairs={{0,1},{1,0},{2,3},{3,2},{4,5},{5,4},{6,7},{7,6},{8,9},{9,8},{10,11... | collective-permute-start | bytes 1572872 | tf_op jit(solution)/shard_map/ppermute | solution.py:351
  150.9 14.0 %collective-permute-start.36 = (bf16[256,1024]{1,0:T(8,128)(2,1)S(1)}, bf16[256,1024]{1,0:T(8,128)(2,1)S(1)}, u32[]{:S(2)}, u32[]{:S(2)}) collective-permute-start(bf16[256,1024]{1,0:T(8,128)(2,1)S(1)} %add_convert_fusion.3), channel_id=1, source_target_pairs={{0,2},{1,3},{2,0},{3,1},{4,6},{5,7},{6,4},{7,5},{8,10},{9,11},{10,... | collective-permute-start | bytes 1572872 | tf_op jit(solution)/shard_map/ppermute | solution.py:351
  168.8 25.9 %collective-permute-start.40 = (bf16[2,2,2,2,32,1024]{5,4,3,2,1,0:T(8,128)(2,1)}, bf16[2,2,2,2,32,1024]{5,4,3,2,1,0:T(8,128)(2,1)}, u32[]{:S(2)}, u32[]{:S(2)}) collective-permute-start(bf16[2,2,2,2,32,1024]{5,4,3,2,1,0:T(8,128)(2,1)} %dynamic-slice_bitcast_fusion), channel_id=1, source_target_pairs={{0,1},{1,0},{2,3},{3,2},{4,5},{5,4},{6,7},{7,6},{8,9},{9,8},{10,11... | collective-permute-start | bytes 3145736 | tf_op jit(solution)/shard_map/ppermute | solution.py:351
  170.6 25.9 %collective-permute-start.39 = (bf16[2,2,128,1024]{3,2,0,1:T(8,128)(2,1)}, bf16[2,2,128,1024]{3,2,0,1:T(8,128)(2,1)}, u32[]{:S(2)}, u32[]{:S(2)}) collective-permute-start(bf16[2,2,128,1024]{3,2,0,1:T(8,128)(2,1)} %copy_bitcast_fusion), channel_id=1, source_target_pairs={{0,16},{1,17},{2,18},{3,19},{4,20},{5,21},{6,22},{7,23},{8,24},{9,... | collective-permute-start | bytes 3145736 | tf_op jit(solution)/shard_map/ppermute | solution.py:351
  177.7 15.1 %collective-permute-start.41 = (bf16[256,1024]{1,0:T(8,128)(2,1)}, bf16[256,1024]{1,0:T(8,128)(2,1)}, u32[]{:S(2)}, u32[]{:S(2)}) collective-permute-start(bf16[256,1024]{1,0:T(8,128)(2,1)} %add_convert_fusion.2), channel_id=1, source_target_pairs={{0,2},{1,3},{2,0},{3,1},{4,6},{5,7},{6,4},{7,5},{8,10},{9,11},{10,... | collective-permute-start | bytes 1572872 | tf_op jit(solution)/shard_map/ppermute | solution.py:351
  180.1 17.5 %collective-permute-start.38 = (bf16[512,256]{1,0:T(8,128)(2,1)}, bf16[512,256]{1,0:T(8,128)(2,1)}, u32[]{:S(2)}, u32[]{:S(2)}) collective-permute-start(bf16[512,256]{1,0:T(8,128)(2,1)} %get-tuple-element.255), channel_id=1, source_target_pairs={{0,2},{1,3},{2,0},{3,1},{4,6},{5,7},{6,4},{7,5},{8,10},{9,11},{10,... | collective-permute-start | bytes 786440 | tf_op jit(solution)/shard_map/ppermute | solution.py:351
  197.7 25.8 %collective-permute-start.47 = (bf16[2,2,2,32,1024]{4,3,1,0,2:T(8,128)(2,1)S(1)}, bf16[2,2,2,32,1024]{4,3,1,0,2:T(8,128)(2,1)S(1)}, u32[]{:S(2)}, u32[]{:S(2)}) collective-permute-start(bf16[2,2,2,32,1024]{4,3,1,0,2:T(8,128)(2,1)S(1)} %dynamic-slice_bitcast_fusion.1), channel_id=1, source_target_pairs={{0,16},{1,17},{2,18},{3,19},{4,20},{5,21},{6,22},{7,23},{8,24},{9,... | collective-permute-start | bytes 1572872 | tf_op jit(solution)/shard_map/ppermute | solution.py:351
  198.3 21.6 %collective-permute-start.44 = (bf16[128,1024]{1,0:T(8,128)(2,1)S(1)}, bf16[128,1024]{1,0:T(8,128)(2,1)S(1)}, u32[]{:S(2)}, u32[]{:S(2)}) collective-permute-start(bf16[128,1024]{1,0:T(8,128)(2,1)S(1)} %get-tuple-element.253), channel_id=1, source_target_pairs={{0,0},{1,8},{2,2},{3,10},{4,4},{5,12},{6,6},{7,14},{8,1},{9,9},{10... | collective-permute-start | bytes 786440 | tf_op jit(solution)/shard_map/ppermute | solution.py:359
  199.0 20.9 %collective-permute-start.45 = (bf16[128,1024]{1,0:T(8,128)(2,1)S(1)}, bf16[128,1024]{1,0:T(8,128)(2,1)S(1)}, u32[]{:S(2)}, u32[]{:S(2)}) collective-permute-start(bf16[128,1024]{1,0:T(8,128)(2,1)S(1)} %get-tuple-element.254), channel_id=1, source_target_pairs={{0,4},{1,12},{2,6},{3,14},{4,0},{5,8},{6,2},{7,10},{8,5},{9,13},{1... | collective-permute-start | bytes 786440 | tf_op jit(solution)/shard_map/ppermute | solution.py:359
  202.6 18.5 %collective-permute-start.43 = (bf16[2,128,1024]{2,1,0:T(8,128)(2,1)S(1)}, bf16[2,128,1024]{2,1,0:T(8,128)(2,1)S(1)}, u32[]{:S(2)}, u32[]{:S(2)}) collective-permute-start(bf16[2,128,1024]{2,1,0:T(8,128)(2,1)S(1)} %dynamic-slice_bitcast_fusion.2), channel_id=1, source_target_pairs={{0,1},{1,0},{2,3},{3,2},{4,5},{5,4},{6,7},{7,6},{8,9},{9,8},{10,11... | collective-permute-start | bytes 1572872 | tf_op jit(solution)/shard_map/ppermute | solution.py:351
  207.7 14.6 %collective-permute-start.42 = (bf16[2,2,2,32,1024]{4,3,2,1,0:T(8,128)(2,1)S(1)}, bf16[2,2,2,32,1024]{4,3,2,1,0:T(8,128)(2,1)S(1)}, u32[]{:S(2)}, u32[]{:S(2)}) collective-permute-start(bf16[2,2,2,32,1024]{4,3,2,1,0:T(8,128)(2,1)S(1)} %dynamic-slice_bitcast_fusion.3), channel_id=1, source_target_pairs={{0,16},{1,17},{2,18},{3,19},{4,20},{5,21},{6,22},{7,23},{8,24},{9,... | collective-permute-start | bytes 1572872 | tf_op jit(solution)/shard_map/ppermute | solution.py:351
  227.6 26.6 %collective-permute-start.54 = (bf16[2,128,1024]{2,1,0:T(8,128)(2,1)S(1)}, bf16[2,128,1024]{2,1,0:T(8,128)(2,1)S(1)}, u32[]{:S(2)}, u32[]{:S(2)}) collective-permute-start(bf16[2,128,1024]{2,1,0:T(8,128)(2,1)S(1)} %fusion.29), channel_id=1, source_target_pairs={{0,4},{1,5},{2,6},{3,7},{4,0},{5,1},{6,2},{7,3},{8,12},{9,13},{10,... | collective-permute-start | bytes 1572872 | tf_op jit(solution)/shard_map/ppermute | solution.py:351
  230.5 15.9 %collective-permute-start.49 = (bf16[2,2,2,32,768]{4,3,2,1,0:T(8,128)(2,1)S(1)}, bf16[2,2,2,32,768]{4,3,2,1,0:T(8,128)(2,1)S(1)}, u32[]{:S(2)}, u32[]{:S(2)}) collective-permute-start(bf16[2,2,2,32,768]{4,3,2,1,0:T(8,128)(2,1)S(1)} %dynamic-slice_bitcast_fusion.5), channel_id=1, source_target_pairs={{0,1},{1,0},{2,3},{3,2},{4,5},{5,4},{6,7},{7,6},{8,9},{9,8},{10,11... | collective-permute-start | bytes 1179656 | tf_op jit(solution)/shard_map/ppermute | solution.py:351
  231.7 15.5 %collective-permute-start.51 = (bf16[2,2,2,32,768]{4,3,2,1,0:T(8,128)(2,1)S(1)}, bf16[2,2,2,32,768]{4,3,2,1,0:T(8,128)(2,1)S(1)}, u32[]{:S(2)}, u32[]{:S(2)}) collective-permute-start(bf16[2,2,2,32,768]{4,3,2,1,0:T(8,128)(2,1)S(1)} %dynamic-slice_bitcast_fusion.4), channel_id=1, source_target_pairs={{0,16},{1,17},{2,18},{3,19},{4,20},{5,21},{6,22},{7,23},{8,24},{9,... | collective-permute-start | bytes 1179656 | tf_op jit(solution)/shard_map/ppermute | solution.py:351
  233.0 24.4 %collective-permute-start.48 = (bf16[256,1024]{1,0:T(8,128)(2,1)S(1)}, bf16[256,1024]{1,0:T(8,128)(2,1)S(1)}, u32[]{:S(2)}, u32[]{:S(2)}) collective-permute-start(bf16[256,1024]{1,0:T(8,128)(2,1)S(1)} %slice.294), channel_id=1, source_target_pairs={{0,2},{1,3},{2,0},{3,1},{4,6},{5,7},{6,4},{7,5},{8,10},{9,11},{10,... | collective-permute-start | bytes 1572872 | tf_op jit(solution)/shard_map/ppermute | solution.py:351
  259.3 20.9 %collective-permute-start.57 = (bf16[2,2,32,768]{3,2,1,0:T(8,128)(2,1)S(1)}, bf16[2,2,32,768]{3,2,1,0:T(8,128)(2,1)S(1)}, u32[]{:S(2)}, u32[]{:S(2)}) collective-permute-start(bf16[2,2,32,768]{3,2,1,0:T(8,128)(2,1)S(1)} %dynamic-slice_bitcast_fusion.11), channel_id=1, source_target_pairs={{0,4},{1,5},{2,6},{3,7},{4,0},{5,1},{6,2},{7,3},{8,12},{9,13},{10,... | collective-permute-start | bytes 589832 | tf_op jit(solution)/shard_map/ppermute | solution.py:351
  259.4 20.8 %collective-permute-start.58 = (bf16[2,32,1024]{2,1,0:T(8,128)(2,1)S(1)}, bf16[2,32,1024]{2,1,0:T(8,128)(2,1)S(1)}, u32[]{:S(2)}, u32[]{:S(2)}) collective-permute-start(bf16[2,32,1024]{2,1,0:T(8,128)(2,1)S(1)} %dynamic-slice_bitcast_fusion.14), channel_id=1, source_target_pairs={{0,4},{1,5},{2,6},{3,7},{4,0},{5,1},{6,2},{7,3},{8,12},{9,13},{10,... | collective-permute-start | bytes 393224 | tf_op jit(solution)/shard_map/ppermute | solution.py:351
  262.4 25.6 %collective-permute-start.55 = (bf16[128,1024]{1,0:T(8,128)(2,1)S(1)}, bf16[128,1024]{1,0:T(8,128)(2,1)S(1)}, u32[]{:S(2)}, u32[]{:S(2)}) collective-permute-start(bf16[128,1024]{1,0:T(8,128)(2,1)S(1)} %get-tuple-element.249), channel_id=1, source_target_pairs={{0,0},{1,8},{2,2},{3,10},{4,4},{5,12},{6,6},{7,14},{8,1},{9,9},{10... | collective-permute-start | bytes 786440 | tf_op jit(solution)/shard_map/ppermute | solution.py:359
  263.1 24.9 %collective-permute-start.56 = (bf16[128,1024]{1,0:T(8,128)(2,1)S(1)}, bf16[128,1024]{1,0:T(8,128)(2,1)S(1)}, u32[]{:S(2)}, u32[]{:S(2)}) collective-permute-start(bf16[128,1024]{1,0:T(8,128)(2,1)S(1)} %get-tuple-element.250), channel_id=1, source_target_pairs={{0,4},{1,12},{2,6},{3,14},{4,0},{5,8},{6,2},{7,10},{8,5},{9,13},{1... | collective-permute-start | bytes 786440 | tf_op jit(solution)/shard_map/ppermute | solution.py:359
  (62 other events, 681.9 us)
where the time goes:
time: 299 us; the launch traced here: 298 us
  waiting for transfers between devices  118 us (39%)
  starting transfers between devices  79.1 us (26%)
  Pallas kernels  42.8 us (14%)
  other arithmetic  26.8 us (9%)
  local copies, waits for them, and re-layouts  20.1 us (7%)
  matrix products  8.27 us (3%)
    ppermute x54, waiting for transfers between devices, swap(): return lax.ppermute(values, AXES, [(i, i ^ mask) for i in range(32)])  106 us
    ppermute x54, starting transfers between devices, swap(): return lax.ppermute(values, AXES, [(i, i ^ mask) for i in range(32)])  63.7 us
    pallas_call x2, Pallas kernels, feed(): pl.pallas_call(feed_kernel, out_shape=(jax.ShapeDtypeStruct((count, hidde...  13.4 us
    ppermute x8, starting transfers between devices, regroup(): return lax.ppermute(values, AXES, pairs)  12.1 us
    pallas_call x1, Pallas kernels, attend_back(): pl.pallas_call(attend_back_kernel, in_specs=[in_smem(), in_smem()] + [in_...  10.6 us
    convert_element_type x16, other arithmetic, low(): return values.astype(jnp.bfloat16)  9.65 us
    ppermute x8, waiting for transfers between devices, regroup(): return lax.ppermute(values, AXES, pairs)  9 us
    pallas_call x1, Pallas kernels, attend(): pl.pallas_call(attend_kernel, in_specs=[in_smem(), in_smem(), in_vmem()],...  8.49 us
  transfers between devices with their start and end apart: 63, of which 27 were waited for; matrix products, arithmetic and copies ran while one was open for 16% of the time, Pallas kernels for 11%

commit v1 on v0

--- a/solution.py
+++ b/solution.py
@@ -667,34 +667,27 @@
 
 
 def feed_kernel(rows, grads, w_up, w_down, bias, activ, grad_up, back, forth, sums):
-    step = rows.shape[0]
-    pieces = w_up.shape[1] // STEP
     sums[...] = jnp.zeros_like(sums)
 
-    def places(number):
-        spot = pl.ds(pl.multiple_of((number // pieces) * step, step), step)
-        return spot, pl.ds(pl.multiple_of((number % pieces) * STEP, STEP), STEP)
-
     def inner(number, unused):
-        spot, unit = places(number)
-        upper = dense(rows[spot], w_up[:, unit]) + bias[:, unit]
+        spot = pl.ds(pl.multiple_of(number * STEP, STEP), STEP)
+        upper = dense(rows[spot], w_up[...]) + bias[...]
         share = 0.5 + 0.5 * lax.erf(upper * (0.5**0.5))
-        activ[spot, unit] = low(upper * share)
+        activ[spot] = low(upper * share)
         slope = share + upper * jnp.exp(-0.5 * upper * upper) * 0.3989422804014327
-        grad = low(dot_t(grads[spot], w_down[unit]) * slope)
-        grad_up[spot, unit] = grad
-        sums[:, unit] += jnp.sum(wide(grad), axis=0, keepdims=True)
+        grad = low(dot_t(grads[spot], w_down[...]) * slope)
+        grad_up[spot] = grad
+        sums[...] += jnp.sum(wide(grad), axis=0, keepdims=True)
         return unused
 
     def outwards(number, unused):
-        spot, unit = places(number)
-        back[spot, unit] = low(dot_t(grad_up[spot], w_up[unit]))
-        forth[spot, unit] = low(dense(activ[spot], w_down[:, unit]))
+        unit = pl.ds(pl.multiple_of(number * STEP, STEP), STEP)
+        back[:, unit] = low(dot_t(grad_up[...], w_up[unit]))
+        forth[:, unit] = low(dense(activ[...], w_down[:, unit]))
         return unused
 
-    count = (rows.shape[0] // step) * pieces
-    lax.fori_loop(0, count, inner, 0)
-    lax.fori_loop(0, count, outwards, 0)
+    lax.fori_loop(0, rows.shape[0] // STEP, inner, 0)
+    lax.fori_loop(0, w_up.shape[0] // STEP, outwards, 0)
 
 
 def feed(rows, grads, w_up, w_down, bias):
@@ -897,8 +890,9 @@
     far, back, grad_qkv, grad_w_out, grad_up, grad_down = tie(
         far, back, grad_qkv, grad_w_out, grad_up, grad_down
     )
-    back = back + wide(far)
-    grad_one = back[:count] + wide(swap(low(back[count:]), Z0))
+    back_own = back[:count] + wide(far[:count])
+    back_other = low(back[count:] + wide(far[count:]))
+    grad_one = back_own + wide(swap(back_other, Z0))
     qkv_near = low(shrink(low(shrink(grad_qkv[:, 0], 3, x, X)), 0, y, Y))
     qkv_far = low(shrink(low(shrink(grad_qkv[:, 1], 0, y, Y)), 2, x, X))
     grads = jnp.stack((grad_down, grad_up.transpose(1, 0, 2, 3, 4).reshape(2, 128, -1)), 1)

time: 299 us -> 297 us (level)
    convert_element_type x16 -> x17, other arithmetic: 9.65 us -> 9.82 us  [low(): return values.astype(jnp.bfloat16)]
where the time goes in v1:
time: 297 us; the launch traced here: 296 us
  waiting for transfers between devices  119 us (40%)
  starting transfers between devices  78.9 us (27%)
  Pallas kernels  40.9 us (14%)
  other arithmetic  26.6 us (9%)
  local copies, waits for them, and re-layouts  20 us (7%)
  matrix products  8.27 us (3%)
    ppermute x54, waiting for transfers between devices, swap(): return lax.ppermute(values, AXES, [(i, i ^ mask) for i in range(32)])  107 us
    ppermute x54, starting transfers between devices, swap(): return lax.ppermute(values, AXES, [(i, i ^ mask) for i in range(32)])  63.7 us
    ppermute x8, starting transfers between devices, regroup(): return lax.ppermute(values, AXES, pairs)  12.1 us
    pallas_call x2, Pallas kernels, feed(): pl.pallas_call(feed_kernel, out_shape=(jax.ShapeDtypeStruct((count, hidde...  11.7 us
    pallas_call x1, Pallas kernels, attend_back(): pl.pallas_call(attend_back_kernel, in_specs=[in_smem(), in_smem()] + [in_...  10.4 us
    convert_element_type x17, other arithmetic, low(): return values.astype(jnp.bfloat16)  9.82 us
    ppermute x8, waiting for transfers between devices, regroup(): return lax.ppermute(values, AXES, pairs)  9 us
    pallas_call x1, Pallas kernels, attend(): pl.pallas_call(attend_kernel, in_specs=[in_smem(), in_smem(), in_vmem()],...  8.49 us
  transfers between devices with their start and end apart: 63, of which 27 were waited for; matrix products, arithmetic and copies ran while one was open for 16% of the time, Pallas kernels for 11%

profile of v1, /device:TPU:0, one launch (start us, length us, event | category | flops | bytes accessed | tf_op | source)
XLA Modules:
  0.0 295.7 jit_solution(14802165529460431734)
XLA Ops:
  2.5 4.1 %collective-permute-start.9 = (bf16[128,1024]{1,0:T(8,128)(2,1)S(1)}, bf16[128,1024]{1,0:T(8,128)(2,1)S(1)}, u32[]{:S(2)}, u32[]{:S(2)}) collective-permute-start(bf16[128,1024]{1,0:T(8,128)(2,1)S(1)} %get-tuple-element.273), channel_id=1, source_target_pairs={{0,4},{1,12},{2,6},{3,14},{4,0},{5,8},{6,2},{7,10},{8,5},{9,13},{1... | collective-permute-start | bytes 786440 | tf_op jit(solution)/shard_map/ppermute | solution.py:359
  13.7 7.0 %collective-permute-done.7 = bf16[32,1024]{1,0:T(8,128)(2,1)S(1)} collective-permute-done((bf16[32,1024]{1,0:T(8,128)(2,1)}, bf16[32,1024]{1,0:T(8,128)(2,1)S(1)}, u32[]{:S(2)}, u32[]{:S(2)}) %collective-permute-start.7) | collective-permute-done | bytes 65568 | tf_op jit(solution)/shard_map/ppermute | solution.py:351
  20.6 2.4 collective-permute-start.6
  23.7 3.2 %collective-permute-start.1 = (bf16[128,1024]{1,0:T(8,128)(2,1)S(1)}, bf16[128,1024]{1,0:T(8,128)(2,1)S(1)}, u32[]{:S(2)}, u32[]{:S(2)}) collective-permute-start(bf16[128,1024]{1,0:T(8,128)(2,1)S(1)} %get-tuple-element.276), channel_id=1, source_target_pairs={{0,4},{1,12},{2,6},{3,14},{4,0},{5,8},{6,2},{7,10},{8,5},{9,13},{1... | collective-permute-start | bytes 786440 | tf_op jit(solution)/shard_map/ppermute | solution.py:359
  28.0 4.2 %collective-permute-start.10 = (bf16[2,2,32,896]{3,2,1,0:T(8,128)(2,1)S(1)}, bf16[2,2,32,896]{3,2,1,0:T(8,128)(2,1)S(1)}, u32[]{:S(2)}, u32[]{:S(2)}) collective-permute-start(bf16[2,2,32,896]{3,2,1,0:T(8,128)(2,1)S(1)} %pad_maximum_fusion.26), channel_id=1, source_target_pairs={{0,4},{1,5},{2,6},{3,7},{4,0},{5,1},{6,2},{7,3},{8,12},{9,13},{10,... | collective-permute-start | bytes 688136 | tf_op jit(solution)/shard_map/ppermute | solution.py:351
  34.3 9.0 %collective-permute-done.1 = bf16[128,1024]{1,0:T(8,128)(2,1)S(1)} collective-permute-done((bf16[128,1024]{1,0:T(8,128)(2,1)S(1)}, bf16[128,1024]{1,0:T(8,128)(2,1)S(1)}, u32[]{:S(2)}, u32[]{:S(2)}) %collective-permute-start.1) | collective-permute-done | bytes 262176 | tf_op jit(solution)/shard_map/ppermute | solution.py:359
  45.8 2.5 collective-permute-done.10
  50.2 3.9 %collective-permute-start.11 = (bf16[2,2,32,896]{3,2,1,0:T(8,128)(2,1)S(1)}, bf16[2,2,32,896]{3,2,1,0:T(8,128)(2,1)S(1)}, u32[]{:S(2)}, u32[]{:S(2)}) collective-permute-start(bf16[2,2,32,896]{3,2,1,0:T(8,128)(2,1)S(1)} %slice_bitcast_fusion.1), channel_id=1, source_target_pairs={{0,1},{1,0},{2,3},{3,2},{4,5},{5,4},{6,7},{7,6},{8,9},{9,8},{10,11... | collective-permute-start | bytes 688136 | tf_op jit(solution)/shard_map/ppermute | solution.py:351
  54.2 3.8 %collective-permute-done.13 = bf16[2,2,32,896]{3,2,1,0:T(8,128)(2,1)S(1)} collective-permute-done((bf16[2,2,32,896]{3,2,1,0:T(8,128)(2,1)S(1)}, bf16[2,2,32,896]{3,2,1,0:T(8,128)(2,1)S(1)}, u32[]{:S(2)}, u32[]{:S(2)}) %collective-permute-start.13) | collective-permute-done | bytes 229408 | tf_op jit(solution)/shard_map/ppermute | solution.py:351
  61.0 5.3 %collective-permute-done.2 = bf16[256,1024]{1,0:T(8,128)(2,1)S(1)} collective-permute-done((bf16[256,1024]{1,0:T(8,128)(2,1)S(1)}, bf16[256,1024]{1,0:T(8,128)(2,1)S(1)}, u32[]{:S(2)}, u32[]{:S(2)}) %collective-permute-start.2) | collective-permute-done | bytes 524320 | tf_op jit(solution)/shard_map/ppermute | solution.py:351
  66.8 4.3 %collective-permute-done.14 = bf16[2,2,2,32,896]{4,3,2,1,0:T(8,128)(2,1)S(1)} collective-permute-done((bf16[2,2,2,32,896]{4,3,2,1,0:T(8,128)(2,1)S(1)}, bf16[2,2,2,32,896]{4,3,2,1,0:T(8,128)(2,1)S(1)}, u32[]{:S(2)}, u32[]{:S(2)}) %collective-permute-start.14) | collective-permute-done | bytes 458784 | tf_op jit(solution)/shard_map/ppermute | solution.py:351
  71.7 2.8 collective-permute-start.22
  84.1 8.5 %attend.1 = (bf16[512,256]{1,0:T(8,128)(2,1)S(1)}, bf16[512,256]{1,0:T(8,128)(2,1)S(1)}, f32[2,1024]{1,0:T(2,128)S(1)}) custom-call(f32[3]{0:T(128)S(1)} %broadcast_multiply_fusion.6.ends, s32[3]{0:T(128)S(1)} %pad_add_fusion.flips, bf16[1024,768]{1,0:T(8,128)(2,1)S(1)} %convolution_convert_fusion.1.mixed), custom_call_target="tpu_custom_call" | custom-call | flops 9663676416 | bytes 4194304 | tf_op jit(solution)/shard_map/attend/pallas_call | solution.py:539
  108.1 10.0 %collective-permute-done.31 = bf16[2,2,2,32,1024]{4,3,1,0,2:T(8,128)(2,1)S(1)} collective-permute-done((bf16[2,2,2,32,1024]{4,3,1,0,2:T(8,128)(2,1)S(1)}, bf16[2,2,2,32,1024]{4,3,1,0,2:T(8,128)(2,1)S(1)}, u32[]{:S(2)}, u32[]{:S(2)}) %collective-permute-start.31) | collective-permute-done | bytes 524320 | tf_op jit(solution)/shard_map/ppermute | solution.py:351
  124.4 7.2 %collective-permute-done.26 = bf16[256,1024]{1,0:T(8,128)(2,1)S(1)} collective-permute-done((bf16[256,1024]{1,0:T(8,128)(2,1)S(1)}, bf16[256,1024]{1,0:T(8,128)(2,1)S(1)}, u32[]{:S(2)}, u32[]{:S(2)}) %collective-permute-start.26) | collective-permute-done | bytes 524320 | tf_op jit(solution)/shard_map/ppermute | solution.py:351
  132.2 2.2 collective-permute-done.28
  136.7 5.8 %feed.3 = (bf16[512,1024]{1,0:T(8,128)(2,1)S(1)}, bf16[512,1024]{1,0:T(8,128)(2,1)S(1)}, bf16[512,1024]{1,0:T(8,128)(2,1)S(1)}, bf16[512,1024]{1,0:T(8,128)(2,1)S(1)}, f32[1,1024]{1,0:T(1,128)S(1)}) custom-call(bf16[512,1024]{1,0:T(8,128)(2,1)S(1)} %collective-permute-done.27.rows.former_far, bf16[512,1024]{1,0:T(8,128)(2,1)S(1)} %collective-permute-done.24.grads.latter_far, ...), custom_call_target="tpu_custom_call" | custom-call | flops 5905580032 | bytes 8388608 | tf_op jit(solution)/shard_map/feed/pallas_call | solution.py:697
  143.1 5.8 %feed.2 = (bf16[512,1024]{1,0:T(8,128)(2,1)S(1)}, bf16[512,1024]{1,0:T(8,128)(2,1)S(1)}, bf16[512,1024]{1,0:T(8,128)(2,1)S(1)}, bf16[512,1024]{1,0:T(8,128)(2,1)S(1)}, f32[1,1024]{1,0:T(1,128)S(1)}) custom-call(bf16[512,1024]{1,0:T(8,128)(2,1)S(1)} %pad_maximum_fusion.6.rows.former_near, bf16[512,1024]{1,0:T(8,128)(2,1)S(1)} %pad_maximum_fusion.4.grads.latter_near, ...), custom_call_target="tpu_custom_call" | custom-call | flops 5905580032 | bytes 8388608 | tf_op jit(solution)/shard_map/feed/pallas_call | solution.py:697
  149.7 3.0 %outer.3 = bf16[1024,1024]{1,0:T(8,128)(2,1)S(1)} custom-call(bf16[512,1024]{1,0:T(8,128)(2,1)S(1)} %pad_maximum_fusion.6.rows.former_near, bf16[512,1024]{1,0:T(8,128)(2,1)S(1)} %collective-permute-done.27.rows.former_far, bf16[512,1024]{1,0:T(8,128)(2,1)S(1)} %get-tuple-element.159.latter_near, bf16[512,1024]{1,0:T(8,128)(2,1)S(1)} %get-tuple-element.160.latter_far), custom_call_target="tpu_custom_call" | custom-call | flops 3221225472 | bytes 6291456 | tf_op jit(solution)/shard_map/outer/pallas_call | solution.py:658
  152.7 3.2 %outer.2 = bf16[1024,1024]{1,0:T(8,128)(2,1)S(1)} custom-call(bf16[512,1024]{1,0:T(8,128)(2,1)S(1)} %get-tuple-element.157.former_near, bf16[512,1024]{1,0:T(8,128)(2,1)S(1)} %get-tuple-element.158.former_far, bf16[512,1024]{1,0:T(8,128)(2,1)S(1)} %pad_maximum_fusion.4.grads.latter_near, bf16[512,1024]{1,0:T(8,128)(2,1)S(1)} %collective-permute-done.24.grads.latter_far), custom_call_target="tpu_custom_call" | custom-call | flops 3221225472 | bytes 6291456 | tf_op jit(solution)/shard_map/outer/pallas_call | solution.py:658
  156.0 7.2 %collective-permute-done.36 = bf16[256,1024]{1,0:T(8,128)(2,1)S(1)} collective-permute-done((bf16[256,1024]{1,0:T(8,128)(2,1)S(1)}, bf16[256,1024]{1,0:T(8,128)(2,1)S(1)}, u32[]{:S(2)}, u32[]{:S(2)}) %collective-permute-start.36) | collective-permute-done | bytes 524320 | tf_op jit(solution)/shard_map/ppermute | solution.py:351
  181.3 9.8 %collective-permute-done.41 = bf16[256,1024]{1,0:T(8,128)(2,1)} collective-permute-done((bf16[256,1024]{1,0:T(8,128)(2,1)}, bf16[256,1024]{1,0:T(8,128)(2,1)}, u32[]{:S(2)}, u32[]{:S(2)}) %collective-permute-start.41) | collective-permute-done | bytes 524320 | tf_op jit(solution)/shard_map/ppermute | solution.py:351
  200.9 3.5 %collective-permute-start.43 = (bf16[2,128,1024]{2,1,0:T(8,128)(2,1)S(1)}, bf16[2,128,1024]{2,1,0:T(8,128)(2,1)S(1)}, u32[]{:S(2)}, u32[]{:S(2)}) collective-permute-start(bf16[2,128,1024]{2,1,0:T(8,128)(2,1)S(1)} %dynamic-slice_bitcast_fusion.2), channel_id=1, source_target_pairs={{0,1},{1,0},{2,3},{3,2},{4,5},{5,4},{6,7},{7,6},{8,9},{9,8},{10,11... | collective-permute-start | bytes 1572872 | tf_op jit(solution)/shard_map/ppermute | solution.py:351
  207.6 10.4 %attend_back.1 = bf16[1024,768]{1,0:T(8,128)(2,1)S(1)} custom-call(f32[3]{0:T(128)S(1)} %broadcast_multiply_fusion.6.ends, s32[3]{0:T(128)S(1)} %pad_add_fusion.flips, bf16[1024,768]{1,0:T(8,128)(2,1)S(1)} %copy-done.4, bf16[512,256]{1,0:T(8,128)(2,1)S(1)} %get-tuple-element.256.near, bf16[512,256]{1,0:T(8,128)(2,1)} %collective-permute-done.38.far, ...), custom_call_target="tpu_custom_call" | custom-call | flops 11811160064 | bytes 6291456 | tf_op jit(solution)/shard_map/attend_back/pallas_call | solution.py:556
  232.2 4.7 %collective-permute-done.53 = bf16[2,2,32,1024]{3,2,1,0:T(8,128)(2,1)S(1)} collective-permute-done((bf16[2,2,32,1024]{3,2,1,0:T(8,128)(2,1)S(1)}, bf16[2,2,32,1024]{3,2,1,0:T(8,128)(2,1)S(1)}, u32[]{:S(2)}, u32[]{:S(2)}) %collective-permute-start.53) | collective-permute-done | bytes 262176 | tf_op jit(solution)/shard_map/ppermute | solution.py:351
  237.0 7.6 %collective-permute-done.49 = bf16[2,2,2,32,768]{4,3,2,1,0:T(8,128)(2,1)S(1)} collective-permute-done((bf16[2,2,2,32,768]{4,3,2,1,0:T(8,128)(2,1)S(1)}, bf16[2,2,2,32,768]{4,3,2,1,0:T(8,128)(2,1)S(1)}, u32[]{:S(2)}, u32[]{:S(2)}) %collective-permute-start.49) | collective-permute-done | bytes 393248 | tf_op jit(solution)/shard_map/ppermute | solution.py:351
  246.6 5.8 %collective-permute-done.54 = bf16[2,128,1024]{2,1,0:T(8,128)(2,1)S(1)} collective-permute-done((bf16[2,128,1024]{2,1,0:T(8,128)(2,1)S(1)}, bf16[2,128,1024]{2,1,0:T(8,128)(2,1)S(1)}, u32[]{:S(2)}, u32[]{:S(2)}) %collective-permute-start.54) | collective-permute-done | bytes 524320 | tf_op jit(solution)/shard_map/ppermute | solution.py:351
  252.6 2.7 collective-permute-done.48
  257.4 3.0 %collective-permute-start.58 = (bf16[2,32,1024]{2,1,0:T(8,128)(2,1)S(1)}, bf16[2,32,1024]{2,1,0:T(8,128)(2,1)S(1)}, u32[]{:S(2)}, u32[]{:S(2)}) collective-permute-start(bf16[2,32,1024]{2,1,0:T(8,128)(2,1)S(1)} %dynamic-slice_bitcast_fusion.14), channel_id=1, source_target_pairs={{0,4},{1,5},{2,6},{3,7},{4,0},{5,1},{6,2},{7,3},{8,12},{9,13},{10,... | collective-permute-start | bytes 393224 | tf_op jit(solution)/shard_map/ppermute | solution.py:351
  261.2 17.2 %collective-permute-done.58 = bf16[2,32,1024]{2,1,0:T(8,128)(2,1)S(1)} collective-permute-done((bf16[2,32,1024]{2,1,0:T(8,128)(2,1)S(1)}, bf16[2,32,1024]{2,1,0:T(8,128)(2,1)S(1)}, u32[]{:S(2)}, u32[]{:S(2)}) %collective-permute-start.58) | collective-permute-done | bytes 131104 | tf_op jit(solution)/shard_map/ppermute | solution.py:351
  279.7 3.1 %all-to-all-start = ((f32[32,1,320]{2,1,0:T(1,128)}), f32[32,1,320]{2,1,0:T(1,128)S(1)}, u32[]{:S(2)}, u32[]{:S(2)}) async-start(f32[32,1,320]{2,1,0:T(1,128)} %copy.94), calls=%async_computation | async-start | bytes 98304 | tf_op jit(solution)/shard_map/all_to_all | solution.py:936
  287.0 3.1 %all-to-all-done = f32[32,1,320]{2,1,0:T(1,128)S(1)} async-done(((f32[32,1,320]{2,1,0:T(1,128)}), f32[32,1,320]{2,1,0:T(1,128)S(1)}, u32[]{:S(2)}, u32[]{:S(2)}) %all-to-all-start) | async-done | bytes 40992 | tf_op jit(solution)/shard_map/all_to_all | solution.py:936
  (337 shorter events, 117.2 us)
Async XLA Ops:
  1.8 25.2 %collective-permute-start.8 = (bf16[128,1024]{1,0:T(8,128)(2,1)S(1)}, bf16[128,1024]{1,0:T(8,128)(2,1)S(1)}, u32[]{:S(2)}, u32[]{:S(2)}) collective-permute-start(bf16[128,1024]{1,0:T(8,128)(2,1)S(1)} %get-tuple-element.274), channel_id=1, source_target_pairs={{0,0},{1,8},{2,2},{3,10},{4,4},{5,12},{6,6},{7,14},{8,1},{9,9},{10... | collective-permute-start | bytes 786440 | tf_op jit(solution)/shard_map/ppermute | solution.py:359
  2.5 24.5 %collective-permute-start.9 = (bf16[128,1024]{1,0:T(8,128)(2,1)S(1)}, bf16[128,1024]{1,0:T(8,128)(2,1)S(1)}, u32[]{:S(2)}, u32[]{:S(2)}) collective-permute-start(bf16[128,1024]{1,0:T(8,128)(2,1)S(1)} %get-tuple-element.273), channel_id=1, source_target_pairs={{0,4},{1,12},{2,6},{3,14},{4,0},{5,8},{6,2},{7,10},{8,5},{9,13},{1... | collective-permute-start | bytes 786440 | tf_op jit(solution)/shard_map/ppermute | solution.py:359
  6.6 14.1 %collective-permute-start.7 = (bf16[32,1024]{1,0:T(8,128)(2,1)}, bf16[32,1024]{1,0:T(8,128)(2,1)S(1)}, u32[]{:S(2)}, u32[]{:S(2)}) collective-permute-start(bf16[32,1024]{1,0:T(8,128)(2,1)} %param.18), channel_id=1, source_target_pairs={{0,4},{1,5},{2,6},{3,7},{4,0},{5,1},{6,2},{7,3},{8,12},{9,13},{10,... | collective-permute-start | bytes 196616 | tf_op jit(solution)/shard_map/ppermute | solution.py:351
  8.6 14.4 %collective-permute-start.4 = (bf16[32,1920]{1,0:T(8,128)(2,1)}, bf16[32,1920]{1,0:T(8,128)(2,1)S(1)}, u32[]{:S(2)}, u32[]{:S(2)}) collective-permute-start(bf16[32,1920]{1,0:T(8,128)(2,1)} %get-tuple-element.108), channel_id=1, source_target_pairs={{0,2},{1,3},{2,0},{3,1},{4,6},{5,7},{6,4},{7,5},{8,10},{9,11},{10,... | collective-permute-start | bytes 368648 | tf_op jit(solution)/shard_map/ppermute | solution.py:351
  23.7 19.6 %collective-permute-start.1 = (bf16[128,1024]{1,0:T(8,128)(2,1)S(1)}, bf16[128,1024]{1,0:T(8,128)(2,1)S(1)}, u32[]{:S(2)}, u32[]{:S(2)}) collective-permute-start(bf16[128,1024]{1,0:T(8,128)(2,1)S(1)} %get-tuple-element.276), channel_id=1, source_target_pairs={{0,4},{1,12},{2,6},{3,14},{4,0},{5,8},{6,2},{7,10},{8,5},{9,13},{1... | collective-permute-start | bytes 786440 | tf_op jit(solution)/shard_map/ppermute | solution.py:359
  28.0 20.3 %collective-permute-start.10 = (bf16[2,2,32,896]{3,2,1,0:T(8,128)(2,1)S(1)}, bf16[2,2,32,896]{3,2,1,0:T(8,128)(2,1)S(1)}, u32[]{:S(2)}, u32[]{:S(2)}) collective-permute-start(bf16[2,2,32,896]{3,2,1,0:T(8,128)(2,1)S(1)} %pad_maximum_fusion.26), channel_id=1, source_target_pairs={{0,4},{1,5},{2,6},{3,7},{4,0},{5,1},{6,2},{7,3},{8,12},{9,13},{10,... | collective-permute-start | bytes 688136 | tf_op jit(solution)/shard_map/ppermute | solution.py:351
  44.1 22.3 %collective-permute-start.2 = (bf16[256,1024]{1,0:T(8,128)(2,1)S(1)}, bf16[256,1024]{1,0:T(8,128)(2,1)S(1)}, u32[]{:S(2)}, u32[]{:S(2)}) collective-permute-start(bf16[256,1024]{1,0:T(8,128)(2,1)S(1)} %fusion.9), channel_id=1, source_target_pairs={{0,2},{1,3},{2,0},{3,1},{4,6},{5,7},{6,4},{7,5},{8,10},{9,11},{10,... | collective-permute-start | bytes 1572872 | tf_op jit(solution)/shard_map/ppermute | solution.py:351
  48.4 18.2 %collective-permute-start.17 = (bf16[128,1024]{1,0:T(8,128)(2,1)S(1)}, bf16[128,1024]{1,0:T(8,128)(2,1)S(1)}, u32[]{:S(2)}, u32[]{:S(2)}) collective-permute-start(bf16[128,1024]{1,0:T(8,128)(2,1)S(1)} %copy-done.25), channel_id=1, source_target_pairs={{0,4},{1,5},{2,6},{3,7},{4,0},{5,1},{6,2},{7,3},{8,12},{9,13},{10,... | collective-permute-start | bytes 786440 | tf_op jit(solution)/shard_map/ppermute | solution.py:351
  71.7 22.9 %collective-permute-start.22 = (bf16[256,1024]{1,0:T(8,128)(2,1)S(1)}, bf16[256,1024]{1,0:T(8,128)(2,1)}, u32[]{:S(2)}, u32[]{:S(2)}) collective-permute-start(bf16[256,1024]{1,0:T(8,128)(2,1)S(1)} %constant_dynamic-update-slice_fusion), channel_id=1, source_target_pairs={{0,2},{1,3},{2,0},{3,1},{4,6},{5,7},{6,4},{7,5},{8,10},{9,11},{10,... | collective-permute-start | bytes 1572872 | tf_op jit(solution)/shard_map/ppermute | solution.py:351
  77.7 19.7 %collective-permute-start.20 = (bf16[2,64,1024]{2,1,0:T(8,128)(2,1)}, bf16[2,64,1024]{2,1,0:T(8,128)(2,1)}, u32[]{:S(2)}, u32[]{:S(2)}) collective-permute-start(bf16[2,64,1024]{2,1,0:T(8,128)(2,1)} %get-tuple-element.268), channel_id=1, source_target_pairs={{0,16},{1,17},{2,18},{3,19},{4,20},{5,21},{6,22},{7,23},{8,24},{9,... | collective-permute-start | bytes 786440 | tf_op jit(solution)/shard_map/ppermute | solution.py:351
  78.5 18.9 %collective-permute-start.21 = (bf16[2,64,1024]{2,1,0:T(8,128)(2,1)}, bf16[2,64,1024]{2,1,0:T(8,128)(2,1)}, u32[]{:S(2)}, u32[]{:S(2)}) collective-permute-start(bf16[2,64,1024]{2,1,0:T(8,128)(2,1)} %get-tuple-element.267), channel_id=1, source_target_pairs={{0,1},{1,0},{2,3},{3,2},{4,5},{5,4},{6,7},{7,6},{8,9},{9,8},{10,11... | collective-permute-start | bytes 786440 | tf_op jit(solution)/shard_map/ppermute | solution.py:351
  80.2 17.2 %collective-permute-start.18 = (bf16[2,2,2,32,1024]{4,3,2,1,0:T(8,128)(2,1)S(1)}, bf16[2,2,2,32,1024]{4,3,2,1,0:T(8,128)(2,1)}, u32[]{:S(2)}, u32[]{:S(2)}) collective-permute-start(bf16[2,2,2,32,1024]{4,3,2,1,0:T(8,128)(2,1)S(1)} %pad_maximum_fusion.11), channel_id=1, source_target_pairs={{0,1},{1,0},{2,3},{3,2},{4,5},{5,4},{6,7},{7,6},{8,9},{9,8},{10,11... | collective-permute-start | bytes 1572872 | tf_op jit(solution)/shard_map/ppermute | solution.py:351
  80.6 16.9 %collective-permute-start.19 = (bf16[2,2,32,1024]{3,2,1,0:T(8,128)(2,1)S(1)}, bf16[2,2,32,1024]{3,2,1,0:T(8,128)(2,1)}, u32[]{:S(2)}, u32[]{:S(2)}) collective-permute-start(bf16[2,2,32,1024]{3,2,1,0:T(8,128)(2,1)S(1)} %pad_maximum_fusion.22), channel_id=1, source_target_pairs={{0,4},{1,5},{2,6},{3,7},{4,0},{5,1},{6,2},{7,3},{8,12},{9,13},{10,... | collective-permute-start | bytes 786440 | tf_op jit(solution)/shard_map/ppermute | solution.py:351
  106.8 13.9 %collective-permute-start.33 = (bf16[2,2,2,32,1024]{4,3,2,1,0:T(8,128)(2,1)S(1)}, bf16[2,2,2,32,1024]{4,3,2,1,0:T(8,128)(2,1)S(1)}, u32[]{:S(2)}, u32[]{:S(2)}) collective-permute-start(bf16[2,2,2,32,1024]{4,3,2,1,0:T(8,128)(2,1)S(1)} %pad_maximum_fusion.16), channel_id=1, source_target_pairs={{0,1},{1,0},{2,3},{3,2},{4,5},{5,4},{6,7},{7,6},{8,9},{9,8},{10,11... | collective-permute-start | bytes 1572872 | tf_op jit(solution)/shard_map/ppermute | solution.py:351
  149.2 14.0 %collective-permute-start.36 = (bf16[256,1024]{1,0:T(8,128)(2,1)S(1)}, bf16[256,1024]{1,0:T(8,128)(2,1)S(1)}, u32[]{:S(2)}, u32[]{:S(2)}) collective-permute-start(bf16[256,1024]{1,0:T(8,128)(2,1)S(1)} %add_convert_fusion.4), channel_id=1, source_target_pairs={{0,2},{1,3},{2,0},{3,1},{4,6},{5,7},{6,4},{7,5},{8,10},{9,11},{10,... | collective-permute-start | bytes 1572872 | tf_op jit(solution)/shard_map/ppermute | solution.py:351
  167.1 25.9 %collective-permute-start.40 = (bf16[2,2,2,2,32,1024]{5,4,3,2,1,0:T(8,128)(2,1)}, bf16[2,2,2,2,32,1024]{5,4,3,2,1,0:T(8,128)(2,1)}, u32[]{:S(2)}, u32[]{:S(2)}) collective-permute-start(bf16[2,2,2,2,32,1024]{5,4,3,2,1,0:T(8,128)(2,1)} %dynamic-slice_bitcast_fusion), channel_id=1, source_target_pairs={{0,1},{1,0},{2,3},{3,2},{4,5},{5,4},{6,7},{7,6},{8,9},{9,8},{10,11... | collective-permute-start | bytes 3145736 | tf_op jit(solution)/shard_map/ppermute | solution.py:351
  168.9 25.9 %collective-permute-start.39 = (bf16[2,2,128,1024]{3,2,0,1:T(8,128)(2,1)}, bf16[2,2,128,1024]{3,2,0,1:T(8,128)(2,1)}, u32[]{:S(2)}, u32[]{:S(2)}) collective-permute-start(bf16[2,2,128,1024]{3,2,0,1:T(8,128)(2,1)} %copy_bitcast_fusion), channel_id=1, source_target_pairs={{0,16},{1,17},{2,18},{3,19},{4,20},{5,21},{6,22},{7,23},{8,24},{9,... | collective-permute-start | bytes 3145736 | tf_op jit(solution)/shard_map/ppermute | solution.py:351
  176.0 15.1 %collective-permute-start.41 = (bf16[256,1024]{1,0:T(8,128)(2,1)}, bf16[256,1024]{1,0:T(8,128)(2,1)}, u32[]{:S(2)}, u32[]{:S(2)}) collective-permute-start(bf16[256,1024]{1,0:T(8,128)(2,1)} %add_convert_fusion.3), channel_id=1, source_target_pairs={{0,2},{1,3},{2,0},{3,1},{4,6},{5,7},{6,4},{7,5},{8,10},{9,11},{10,... | collective-permute-start | bytes 1572872 | tf_op jit(solution)/shard_map/ppermute | solution.py:351
  178.5 17.5 %collective-permute-start.38 = (bf16[512,256]{1,0:T(8,128)(2,1)}, bf16[512,256]{1,0:T(8,128)(2,1)}, u32[]{:S(2)}, u32[]{:S(2)}) collective-permute-start(bf16[512,256]{1,0:T(8,128)(2,1)} %get-tuple-element.255), channel_id=1, source_target_pairs={{0,2},{1,3},{2,0},{3,1},{4,6},{5,7},{6,4},{7,5},{8,10},{9,11},{10,... | collective-permute-start | bytes 786440 | tf_op jit(solution)/shard_map/ppermute | solution.py:351
  196.0 25.8 %collective-permute-start.47 = (bf16[2,2,2,32,1024]{4,3,1,0,2:T(8,128)(2,1)S(1)}, bf16[2,2,2,32,1024]{4,3,1,0,2:T(8,128)(2,1)S(1)}, u32[]{:S(2)}, u32[]{:S(2)}) collective-permute-start(bf16[2,2,2,32,1024]{4,3,1,0,2:T(8,128)(2,1)S(1)} %dynamic-slice_bitcast_fusion.1), channel_id=1, source_target_pairs={{0,16},{1,17},{2,18},{3,19},{4,20},{5,21},{6,22},{7,23},{8,24},{9,... | collective-permute-start | bytes 1572872 | tf_op jit(solution)/shard_map/ppermute | solution.py:351
  196.6 21.4 %collective-permute-start.44 = (bf16[128,1024]{1,0:T(8,128)(2,1)S(1)}, bf16[128,1024]{1,0:T(8,128)(2,1)S(1)}, u32[]{:S(2)}, u32[]{:S(2)}) collective-permute-start(bf16[128,1024]{1,0:T(8,128)(2,1)S(1)} %get-tuple-element.253), channel_id=1, source_target_pairs={{0,0},{1,8},{2,2},{3,10},{4,4},{5,12},{6,6},{7,14},{8,1},{9,9},{10... | collective-permute-start | bytes 786440 | tf_op jit(solution)/shard_map/ppermute | solution.py:359
  197.3 20.7 %collective-permute-start.45 = (bf16[128,1024]{1,0:T(8,128)(2,1)S(1)}, bf16[128,1024]{1,0:T(8,128)(2,1)S(1)}, u32[]{:S(2)}, u32[]{:S(2)}) collective-permute-start(bf16[128,1024]{1,0:T(8,128)(2,1)S(1)} %get-tuple-element.254), channel_id=1, source_target_pairs={{0,4},{1,12},{2,6},{3,14},{4,0},{5,8},{6,2},{7,10},{8,5},{9,13},{1... | collective-permute-start | bytes 786440 | tf_op jit(solution)/shard_map/ppermute | solution.py:359
  200.9 18.5 %collective-permute-start.43 = (bf16[2,128,1024]{2,1,0:T(8,128)(2,1)S(1)}, bf16[2,128,1024]{2,1,0:T(8,128)(2,1)S(1)}, u32[]{:S(2)}, u32[]{:S(2)}) collective-permute-start(bf16[2,128,1024]{2,1,0:T(8,128)(2,1)S(1)} %dynamic-slice_bitcast_fusion.2), channel_id=1, source_target_pairs={{0,1},{1,0},{2,3},{3,2},{4,5},{5,4},{6,7},{7,6},{8,9},{9,8},{10,11... | collective-permute-start | bytes 1572872 | tf_op jit(solution)/shard_map/ppermute | solution.py:351
  206.0 14.5 %collective-permute-start.42 = (bf16[2,2,2,32,1024]{4,3,2,1,0:T(8,128)(2,1)S(1)}, bf16[2,2,2,32,1024]{4,3,2,1,0:T(8,128)(2,1)S(1)}, u32[]{:S(2)}, u32[]{:S(2)}) collective-permute-start(bf16[2,2,2,32,1024]{4,3,2,1,0:T(8,128)(2,1)S(1)} %dynamic-slice_bitcast_fusion.3), channel_id=1, source_target_pairs={{0,16},{1,17},{2,18},{3,19},{4,20},{5,21},{6,22},{7,23},{8,24},{9,... | collective-permute-start | bytes 1572872 | tf_op jit(solution)/shard_map/ppermute | solution.py:351
  225.9 26.5 %collective-permute-start.54 = (bf16[2,128,1024]{2,1,0:T(8,128)(2,1)S(1)}, bf16[2,128,1024]{2,1,0:T(8,128)(2,1)S(1)}, u32[]{:S(2)}, u32[]{:S(2)}) collective-permute-start(bf16[2,128,1024]{2,1,0:T(8,128)(2,1)S(1)} %fusion.29), channel_id=1, source_target_pairs={{0,4},{1,5},{2,6},{3,7},{4,0},{5,1},{6,2},{7,3},{8,12},{9,13},{10,... | collective-permute-start | bytes 1572872 | tf_op jit(solution)/shard_map/ppermute | solution.py:351
  228.8 15.9 %collective-permute-start.49 = (bf16[2,2,2,32,768]{4,3,2,1,0:T(8,128)(2,1)S(1)}, bf16[2,2,2,32,768]{4,3,2,1,0:T(8,128)(2,1)S(1)}, u32[]{:S(2)}, u32[]{:S(2)}) collective-permute-start(bf16[2,2,2,32,768]{4,3,2,1,0:T(8,128)(2,1)S(1)} %dynamic-slice_bitcast_fusion.5), channel_id=1, source_target_pairs={{0,1},{1,0},{2,3},{3,2},{4,5},{5,4},{6,7},{7,6},{8,9},{9,8},{10,11... | collective-permute-start | bytes 1179656 | tf_op jit(solution)/shard_map/ppermute | solution.py:351
  230.0 15.5 %collective-permute-start.51 = (bf16[2,2,2,32,768]{4,3,2,1,0:T(8,128)(2,1)S(1)}, bf16[2,2,2,32,768]{4,3,2,1,0:T(8,128)(2,1)S(1)}, u32[]{:S(2)}, u32[]{:S(2)}) collective-permute-start(bf16[2,2,2,32,768]{4,3,2,1,0:T(8,128)(2,1)S(1)} %dynamic-slice_bitcast_fusion.4), channel_id=1, source_target_pairs={{0,16},{1,17},{2,18},{3,19},{4,20},{5,21},{6,22},{7,23},{8,24},{9,... | collective-permute-start | bytes 1179656 | tf_op jit(solution)/shard_map/ppermute | solution.py:351
  230.9 24.4 %collective-permute-start.48 = (bf16[256,1024]{1,0:T(8,128)(2,1)S(1)}, bf16[256,1024]{1,0:T(8,128)(2,1)S(1)}, u32[]{:S(2)}, u32[]{:S(2)}) collective-permute-start(bf16[256,1024]{1,0:T(8,128)(2,1)S(1)} %add_convert_fusion.1), channel_id=1, source_target_pairs={{0,2},{1,3},{2,0},{3,1},{4,6},{5,7},{6,4},{7,5},{8,10},{9,11},{10,... | collective-permute-start | bytes 1572872 | tf_op jit(solution)/shard_map/ppermute | solution.py:351
  257.3 21.1 %collective-permute-start.57 = (bf16[2,2,32,768]{3,2,1,0:T(8,128)(2,1)S(1)}, bf16[2,2,32,768]{3,2,1,0:T(8,128)(2,1)S(1)}, u32[]{:S(2)}, u32[]{:S(2)}) collective-permute-start(bf16[2,2,32,768]{3,2,1,0:T(8,128)(2,1)S(1)} %dynamic-slice_bitcast_fusion.11), channel_id=1, source_target_pairs={{0,4},{1,5},{2,6},{3,7},{4,0},{5,1},{6,2},{7,3},{8,12},{9,13},{10,... | collective-permute-start | bytes 589832 | tf_op jit(solution)/shard_map/ppermute | solution.py:351
  257.4 21.0 %collective-permute-start.58 = (bf16[2,32,1024]{2,1,0:T(8,128)(2,1)S(1)}, bf16[2,32,1024]{2,1,0:T(8,128)(2,1)S(1)}, u32[]{:S(2)}, u32[]{:S(2)}) collective-permute-start(bf16[2,32,1024]{2,1,0:T(8,128)(2,1)S(1)} %dynamic-slice_bitcast_fusion.14), channel_id=1, source_target_pairs={{0,4},{1,5},{2,6},{3,7},{4,0},{5,1},{6,2},{7,3},{8,12},{9,13},{10,... | collective-permute-start | bytes 393224 | tf_op jit(solution)/shard_map/ppermute | solution.py:351
  260.4 25.5 %collective-permute-start.55 = (bf16[128,1024]{1,0:T(8,128)(2,1)S(1)}, bf16[128,1024]{1,0:T(8,128)(2,1)S(1)}, u32[]{:S(2)}, u32[]{:S(2)}) collective-permute-start(bf16[128,1024]{1,0:T(8,128)(2,1)S(1)} %get-tuple-element.249), channel_id=1, source_target_pairs={{0,0},{1,8},{2,2},{3,10},{4,4},{5,12},{6,6},{7,14},{8,1},{9,9},{10... | collective-permute-start | bytes 786440 | tf_op jit(solution)/shard_map/ppermute | solution.py:359
  261.1 24.8 %collective-permute-start.56 = (bf16[128,1024]{1,0:T(8,128)(2,1)S(1)}, bf16[128,1024]{1,0:T(8,128)(2,1)S(1)}, u32[]{:S(2)}, u32[]{:S(2)}) collective-permute-start(bf16[128,1024]{1,0:T(8,128)(2,1)S(1)} %get-tuple-element.250), channel_id=1, source_target_pairs={{0,4},{1,12},{2,6},{3,14},{4,0},{5,8},{6,2},{7,10},{8,5},{9,13},{1... | collective-permute-start | bytes 786440 | tf_op jit(solution)/shard_map/ppermute | solution.py:359
  (62 other events, 677.0 us)

commit v2 on v1

--- a/solution.py
+++ b/solution.py
@@ -669,25 +669,21 @@
 def feed_kernel(rows, grads, w_up, w_down, bias, activ, grad_up, back, forth, sums):
     sums[...] = jnp.zeros_like(sums)
 
-    def inner(number, unused):
+    def block(number, unused):
         spot = pl.ds(pl.multiple_of(number * STEP, STEP), STEP)
         upper = dense(rows[spot], w_up[...]) + bias[...]
         share = 0.5 + 0.5 * lax.erf(upper * (0.5**0.5))
-        activ[spot] = low(upper * share)
+        act = low(upper * share)
         slope = share + upper * jnp.exp(-0.5 * upper * upper) * 0.3989422804014327
         grad = low(dot_t(grads[spot], w_down[...]) * slope)
+        activ[spot] = act
         grad_up[spot] = grad
         sums[...] += jnp.sum(wide(grad), axis=0, keepdims=True)
+        back[spot] = low(dot_t(grad, w_up[...]))
+        forth[spot] = low(dense(act, w_down[...]))
         return unused
 
-    def outwards(number, unused):
-        unit = pl.ds(pl.multiple_of(number * STEP, STEP), STEP)
-        back[:, unit] = low(dot_t(grad_up[...], w_up[unit]))
-        forth[:, unit] = low(dense(activ[...], w_down[:, unit]))
-        return unused
-
-    lax.fori_loop(0, rows.shape[0] // STEP, inner, 0)
-    lax.fori_loop(0, w_up.shape[0] // STEP, outwards, 0)
+    lax.fori_loop(0, rows.shape[0] // STEP, block, 0)
 
 
 def feed(rows, grads, w_up, w_down, bias):

time: 297 us -> 304 us (1.024); the launches traced: 296 us -> 300 us
  Pallas kernels: 40.9 us -> 51 us
  waiting for transfers between devices: 119 us -> 111 us
    pallas_call x2, Pallas kernels: 6.22 us -> 17.3 us  [outer(): pl.pallas_call(outer_kernel, out_shape=jax.ShapeDtypeStruct((rows, column...]
    ppermute x54, waiting for transfers between devices: 107 us -> 98.9 us  [swap(): return lax.ppermute(values, AXES, [(i, i ^ mask) for i in range(32)])]
  transfers between devices with their start and end apart: 63 -> 63, of which waited for: 27 -> 25; matrix products, arithmetic and copies ran while one was open for 16% -> 16% of each run, Pallas kernels for 11% -> 15%
where the time goes in v2:
time: 304 us; the launch traced here: 300 us
  waiting for transfers between devices  111 us (37%)
  starting transfers between devices  79.7 us (26%)
  Pallas kernels  51 us (17%)
  other arithmetic  26.6 us (9%)
  local copies, waits for them, and re-layouts  20.6 us (7%)
  matrix products  8.27 us (3%)
    ppermute x54, waiting for transfers between devices, swap(): return lax.ppermute(values, AXES, [(i, i ^ mask) for i in range(32)])  98.9 us
    ppermute x54, starting transfers between devices, swap(): return lax.ppermute(values, AXES, [(i, i ^ mask) for i in range(32)])  63.8 us
    pallas_call x2, Pallas kernels, outer(): pl.pallas_call(outer_kernel, out_shape=jax.ShapeDtypeStruct((rows, column...  17.3 us
    ppermute x8, starting transfers between devices, regroup(): return lax.ppermute(values, AXES, pairs)  12.8 us
    pallas_call x2, Pallas kernels, feed(): pl.pallas_call(feed_kernel, out_shape=(jax.ShapeDtypeStruct((count, hidde...  10.6 us
    pallas_call x1, Pallas kernels, attend_back(): pl.pallas_call(attend_back_kernel, in_specs=[in_smem(), in_smem()] + [in_...  10.4 us
    convert_element_type x17, other arithmetic, low(): return values.astype(jnp.bfloat16)  9.81 us
    ppermute x8, waiting for transfers between devices, regroup(): return lax.ppermute(values, AXES, pairs)  9 us
  transfers between devices with their start and end apart: 63, of which 25 were waited for; matrix products, arithmetic and copies ran while one was open for 16% of the time, Pallas kernels for 15%

profile of v2, /device:TPU:0, one launch (start us, length us, event | category | flops | bytes accessed | tf_op | source)
XLA Modules:
  0.0 299.6 jit_solution(16421762258952145078)
XLA Ops:
  2.5 4.1 %collective-permute-start.9 = (bf16[128,1024]{1,0:T(8,128)(2,1)S(1)}, bf16[128,1024]{1,0:T(8,128)(2,1)S(1)}, u32[]{:S(2)}, u32[]{:S(2)}) collective-permute-start(bf16[128,1024]{1,0:T(8,128)(2,1)S(1)} %get-tuple-element.273), channel_id=1, source_target_pairs={{0,4},{1,12},{2,6},{3,14},{4,0},{5,8},{6,2},{7,10},{8,5},{9,13},{1... | collective-permute-start | bytes 786440 | tf_op jit(solution)/shard_map/ppermute | solution.py:359
  13.7 7.0 %collective-permute-done.7 = bf16[32,1024]{1,0:T(8,128)(2,1)S(1)} collective-permute-done((bf16[32,1024]{1,0:T(8,128)(2,1)}, bf16[32,1024]{1,0:T(8,128)(2,1)S(1)}, u32[]{:S(2)}, u32[]{:S(2)}) %collective-permute-start.7) | collective-permute-done | bytes 65568 | tf_op jit(solution)/shard_map/ppermute | solution.py:351
  20.6 2.4 collective-permute-start.6
  23.7 3.2 %collective-permute-start.1 = (bf16[128,1024]{1,0:T(8,128)(2,1)S(1)}, bf16[128,1024]{1,0:T(8,128)(2,1)S(1)}, u32[]{:S(2)}, u32[]{:S(2)}) collective-permute-start(bf16[128,1024]{1,0:T(8,128)(2,1)S(1)} %get-tuple-element.276), channel_id=1, source_target_pairs={{0,4},{1,12},{2,6},{3,14},{4,0},{5,8},{6,2},{7,10},{8,5},{9,13},{1... | collective-permute-start | bytes 786440 | tf_op jit(solution)/shard_map/ppermute | solution.py:359
  28.0 4.2 %collective-permute-start.10 = (bf16[2,2,32,896]{3,2,1,0:T(8,128)(2,1)S(1)}, bf16[2,2,32,896]{3,2,1,0:T(8,128)(2,1)S(1)}, u32[]{:S(2)}, u32[]{:S(2)}) collective-permute-start(bf16[2,2,32,896]{3,2,1,0:T(8,128)(2,1)S(1)} %pad_maximum_fusion.26), channel_id=1, source_target_pairs={{0,4},{1,5},{2,6},{3,7},{4,0},{5,1},{6,2},{7,3},{8,12},{9,13},{10,... | collective-permute-start | bytes 688136 | tf_op jit(solution)/shard_map/ppermute | solution.py:351
  34.3 9.0 %collective-permute-done.1 = bf16[128,1024]{1,0:T(8,128)(2,1)S(1)} collective-permute-done((bf16[128,1024]{1,0:T(8,128)(2,1)S(1)}, bf16[128,1024]{1,0:T(8,128)(2,1)S(1)}, u32[]{:S(2)}, u32[]{:S(2)}) %collective-permute-start.1) | collective-permute-done | bytes 262176 | tf_op jit(solution)/shard_map/ppermute | solution.py:359
  45.8 2.5 collective-permute-done.10
  50.2 3.9 %collective-permute-start.11 = (bf16[2,2,32,896]{3,2,1,0:T(8,128)(2,1)S(1)}, bf16[2,2,32,896]{3,2,1,0:T(8,128)(2,1)S(1)}, u32[]{:S(2)}, u32[]{:S(2)}) collective-permute-start(bf16[2,2,32,896]{3,2,1,0:T(8,128)(2,1)S(1)} %slice_bitcast_fusion.1), channel_id=1, source_target_pairs={{0,1},{1,0},{2,3},{3,2},{4,5},{5,4},{6,7},{7,6},{8,9},{9,8},{10,11... | collective-permute-start | bytes 688136 | tf_op jit(solution)/shard_map/ppermute | solution.py:351
  54.2 3.8 %collective-permute-done.13 = bf16[2,2,32,896]{3,2,1,0:T(8,128)(2,1)S(1)} collective-permute-done((bf16[2,2,32,896]{3,2,1,0:T(8,128)(2,1)S(1)}, bf16[2,2,32,896]{3,2,1,0:T(8,128)(2,1)S(1)}, u32[]{:S(2)}, u32[]{:S(2)}) %collective-permute-start.13) | collective-permute-done | bytes 229408 | tf_op jit(solution)/shard_map/ppermute | solution.py:351
  61.0 5.3 %collective-permute-done.2 = bf16[256,1024]{1,0:T(8,128)(2,1)S(1)} collective-permute-done((bf16[256,1024]{1,0:T(8,128)(2,1)S(1)}, bf16[256,1024]{1,0:T(8,128)(2,1)S(1)}, u32[]{:S(2)}, u32[]{:S(2)}) %collective-permute-start.2) | collective-permute-done | bytes 524320 | tf_op jit(solution)/shard_map/ppermute | solution.py:351
  66.8 4.3 %collective-permute-done.14 = bf16[2,2,2,32,896]{4,3,2,1,0:T(8,128)(2,1)S(1)} collective-permute-done((bf16[2,2,2,32,896]{4,3,2,1,0:T(8,128)(2,1)S(1)}, bf16[2,2,2,32,896]{4,3,2,1,0:T(8,128)(2,1)S(1)}, u32[]{:S(2)}, u32[]{:S(2)}) %collective-permute-start.14) | collective-permute-done | bytes 458784 | tf_op jit(solution)/shard_map/ppermute | solution.py:351
  71.7 2.8 collective-permute-start.22
  84.1 8.6 %attend.1 = (bf16[512,256]{1,0:T(8,128)(2,1)S(1)}, bf16[512,256]{1,0:T(8,128)(2,1)S(1)}, f32[2,1024]{1,0:T(2,128)S(1)}) custom-call(f32[3]{0:T(128)S(1)} %broadcast_multiply_fusion.6.ends, s32[3]{0:T(128)S(1)} %pad_add_fusion.flips, bf16[1024,768]{1,0:T(8,128)(2,1)S(1)} %convolution_convert_fusion.1.mixed), custom_call_target="tpu_custom_call" | custom-call | flops 9663676416 | bytes 4194304 | tf_op jit(solution)/shard_map/attend/pallas_call | solution.py:539
  108.2 10.0 %collective-permute-done.31 = bf16[2,2,2,32,1024]{4,3,1,0,2:T(8,128)(2,1)S(1)} collective-permute-done((bf16[2,2,2,32,1024]{4,3,1,0,2:T(8,128)(2,1)S(1)}, bf16[2,2,2,32,1024]{4,3,1,0,2:T(8,128)(2,1)S(1)}, u32[]{:S(2)}, u32[]{:S(2)}) %collective-permute-start.31) | collective-permute-done | bytes 524320 | tf_op jit(solution)/shard_map/ppermute | solution.py:351
  124.5 7.2 %collective-permute-done.26 = bf16[256,1024]{1,0:T(8,128)(2,1)S(1)} collective-permute-done((bf16[256,1024]{1,0:T(8,128)(2,1)S(1)}, bf16[256,1024]{1,0:T(8,128)(2,1)S(1)}, u32[]{:S(2)}, u32[]{:S(2)}) %collective-permute-start.26) | collective-permute-done | bytes 524320 | tf_op jit(solution)/shard_map/ppermute | solution.py:351
  136.8 5.3 %feed.3 = (bf16[512,1024]{1,0:T(8,128)(2,1)S(1)}, bf16[512,1024]{1,0:T(8,128)(2,1)S(1)}, bf16[512,1024]{1,0:T(8,128)(2,1)S(1)}, bf16[512,1024]{1,0:T(8,128)(2,1)S(1)}, f32[1,1024]{1,0:T(1,128)S(1)}) custom-call(bf16[512,1024]{1,0:T(8,128)(2,1)S(1)} %collective-permute-done.27.rows.former_far, bf16[512,1024]{1,0:T(8,128)(2,1)S(1)} %collective-permute-done.24.grads.latter_far, ...), custom_call_target="tpu_custom_call" | custom-call | flops 5905580032 | bytes 8388608 | tf_op jit(solution)/shard_map/feed/pallas_call | solution.py:693
  142.7 5.3 %feed.2 = (bf16[512,1024]{1,0:T(8,128)(2,1)S(1)}, bf16[512,1024]{1,0:T(8,128)(2,1)S(1)}, bf16[512,1024]{1,0:T(8,128)(2,1)S(1)}, bf16[512,1024]{1,0:T(8,128)(2,1)S(1)}, f32[1,1024]{1,0:T(1,128)S(1)}) custom-call(bf16[512,1024]{1,0:T(8,128)(2,1)S(1)} %pad_maximum_fusion.6.rows.former_near, bf16[512,1024]{1,0:T(8,128)(2,1)S(1)} %pad_maximum_fusion.4.grads.latter_near, ...), custom_call_target="tpu_custom_call" | custom-call | flops 5905580032 | bytes 8388608 | tf_op jit(solution)/shard_map/feed/pallas_call | solution.py:693
  148.7 3.0 %outer.3 = bf16[1024,1024]{1,0:T(8,128)(2,1)S(1)} custom-call(bf16[512,1024]{1,0:T(8,128)(2,1)S(1)} %pad_maximum_fusion.6.rows.former_near, bf16[512,1024]{1,0:T(8,128)(2,1)S(1)} %collective-permute-done.27.rows.former_far, bf16[512,1024]{1,0:T(8,128)(2,1)S(1)} %get-tuple-element.159.latter_near, bf16[512,1024]{1,0:T(8,128)(2,1)S(1)} %get-tuple-element.160.latter_far), custom_call_target="tpu_custom_call" | custom-call | flops 3221225472 | bytes 6291456 | tf_op jit(solution)/shard_map/outer/pallas_call | solution.py:658
  151.7 14.3 %outer.2 = bf16[1024,1024]{1,0:T(8,128)(2,1)S(1)} custom-call(bf16[512,1024]{1,0:T(8,128)(2,1)S(1)} %get-tuple-element.157.former_near, bf16[512,1024]{1,0:T(8,128)(2,1)S(1)} %get-tuple-element.158.former_far, bf16[512,1024]{1,0:T(8,128)(2,1)S(1)} %pad_maximum_fusion.4.grads.latter_near, bf16[512,1024]{1,0:T(8,128)(2,1)S(1)} %collective-permute-done.24.grads.latter_far), custom_call_target="tpu_custom_call" | custom-call | flops 3221225472 | bytes 6291456 | tf_op jit(solution)/shard_map/outer/pallas_call | solution.py:658
  184.8 9.8 %collective-permute-done.41 = bf16[256,1024]{1,0:T(8,128)(2,1)} collective-permute-done((bf16[256,1024]{1,0:T(8,128)(2,1)}, bf16[256,1024]{1,0:T(8,128)(2,1)}, u32[]{:S(2)}, u32[]{:S(2)}) %collective-permute-start.41) | collective-permute-done | bytes 524320 | tf_op jit(solution)/shard_map/ppermute | solution.py:351
  200.8 2.6 collective-permute-start.45
  205.0 3.5 %collective-permute-start.43 = (bf16[2,128,1024]{2,1,0:T(8,128)(2,1)S(1)}, bf16[2,128,1024]{2,1,0:T(8,128)(2,1)S(1)}, u32[]{:S(2)}, u32[]{:S(2)}) collective-permute-start(bf16[2,128,1024]{2,1,0:T(8,128)(2,1)S(1)} %dynamic-slice_bitcast_fusion.2), channel_id=1, source_target_pairs={{0,1},{1,0},{2,3},{3,2},{4,5},{5,4},{6,7},{7,6},{8,9},{9,8},{10,11... | collective-permute-start | bytes 1572872 | tf_op jit(solution)/shard_map/ppermute | solution.py:351
  211.7 10.4 %attend_back.1 = bf16[1024,768]{1,0:T(8,128)(2,1)S(1)} custom-call(f32[3]{0:T(128)S(1)} %broadcast_multiply_fusion.6.ends, s32[3]{0:T(128)S(1)} %pad_add_fusion.flips, bf16[1024,768]{1,0:T(8,128)(2,1)S(1)} %copy-done.4, bf16[512,256]{1,0:T(8,128)(2,1)S(1)} %get-tuple-element.256.near, bf16[512,256]{1,0:T(8,128)(2,1)} %collective-permute-done.38.far, ...), custom_call_target="tpu_custom_call" | custom-call | flops 11811160064 | bytes 6291456 | tf_op jit(solution)/shard_map/attend_back/pallas_call | solution.py:556
  229.3 2.6 collective-permute-start.54
  236.0 5.2 %collective-permute-done.53 = bf16[2,2,32,1024]{3,2,1,0:T(8,128)(2,1)S(1)} collective-permute-done((bf16[2,2,32,1024]{3,2,1,0:T(8,128)(2,1)S(1)}, bf16[2,2,32,1024]{3,2,1,0:T(8,128)(2,1)S(1)}, u32[]{:S(2)}, u32[]{:S(2)}) %collective-permute-start.53) | collective-permute-done | bytes 262176 | tf_op jit(solution)/shard_map/ppermute | solution.py:351
  241.3 7.6 %collective-permute-done.49 = bf16[2,2,2,32,768]{4,3,2,1,0:T(8,128)(2,1)S(1)} collective-permute-done((bf16[2,2,2,32,768]{4,3,2,1,0:T(8,128)(2,1)S(1)}, bf16[2,2,2,32,768]{4,3,2,1,0:T(8,128)(2,1)S(1)}, u32[]{:S(2)}, u32[]{:S(2)}) %collective-permute-start.49) | collective-permute-done | bytes 393248 | tf_op jit(solution)/shard_map/ppermute | solution.py:351
  250.7 5.3 %collective-permute-done.54 = bf16[2,128,1024]{2,1,0:T(8,128)(2,1)S(1)} collective-permute-done((bf16[2,128,1024]{2,1,0:T(8,128)(2,1)S(1)}, bf16[2,128,1024]{2,1,0:T(8,128)(2,1)S(1)}, u32[]{:S(2)}, u32[]{:S(2)}) %collective-permute-start.54) | collective-permute-done | bytes 524320 | tf_op jit(solution)/shard_map/ppermute | solution.py:351
  256.2 2.3 collective-permute-done.48
  260.6 3.0 collective-permute-start.58
  264.4 17.6 %collective-permute-done.58 = bf16[2,32,1024]{2,1,0:T(8,128)(2,1)S(1)} collective-permute-done((bf16[2,32,1024]{2,1,0:T(8,128)(2,1)S(1)}, bf16[2,32,1024]{2,1,0:T(8,128)(2,1)S(1)}, u32[]{:S(2)}, u32[]{:S(2)}) %collective-permute-start.58) | collective-permute-done | bytes 131104 | tf_op jit(solution)/shard_map/ppermute | solution.py:351
  283.4 3.1 %all-to-all-start = ((f32[32,1,320]{2,1,0:T(1,128)}), f32[32,1,320]{2,1,0:T(1,128)S(1)}, u32[]{:S(2)}, u32[]{:S(2)}) async-start(f32[32,1,320]{2,1,0:T(1,128)} %copy.94), calls=%async_computation | async-start | bytes 98304 | tf_op jit(solution)/shard_map/all_to_all | solution.py:932
  290.6 3.1 %all-to-all-done = f32[32,1,320]{2,1,0:T(1,128)S(1)} async-done(((f32[32,1,320]{2,1,0:T(1,128)}), f32[32,1,320]{2,1,0:T(1,128)S(1)}, u32[]{:S(2)}, u32[]{:S(2)}) %all-to-all-start) | async-done | bytes 40992 | tf_op jit(solution)/shard_map/all_to_all | solution.py:932
  (337 shorter events, 114.8 us)
Async XLA Ops:
  1.8 25.2 %collective-permute-start.8 = (bf16[128,1024]{1,0:T(8,128)(2,1)S(1)}, bf16[128,1024]{1,0:T(8,128)(2,1)S(1)}, u32[]{:S(2)}, u32[]{:S(2)}) collective-permute-start(bf16[128,1024]{1,0:T(8,128)(2,1)S(1)} %get-tuple-element.274), channel_id=1, source_target_pairs={{0,0},{1,8},{2,2},{3,10},{4,4},{5,12},{6,6},{7,14},{8,1},{9,9},{10... | collective-permute-start | bytes 786440 | tf_op jit(solution)/shard_map/ppermute | solution.py:359
  2.5 24.5 %collective-permute-start.9 = (bf16[128,1024]{1,0:T(8,128)(2,1)S(1)}, bf16[128,1024]{1,0:T(8,128)(2,1)S(1)}, u32[]{:S(2)}, u32[]{:S(2)}) collective-permute-start(bf16[128,1024]{1,0:T(8,128)(2,1)S(1)} %get-tuple-element.273), channel_id=1, source_target_pairs={{0,4},{1,12},{2,6},{3,14},{4,0},{5,8},{6,2},{7,10},{8,5},{9,13},{1... | collective-permute-start | bytes 786440 | tf_op jit(solution)/shard_map/ppermute | solution.py:359
  6.6 14.1 %collective-permute-start.7 = (bf16[32,1024]{1,0:T(8,128)(2,1)}, bf16[32,1024]{1,0:T(8,128)(2,1)S(1)}, u32[]{:S(2)}, u32[]{:S(2)}) collective-permute-start(bf16[32,1024]{1,0:T(8,128)(2,1)} %param.18), channel_id=1, source_target_pairs={{0,4},{1,5},{2,6},{3,7},{4,0},{5,1},{6,2},{7,3},{8,12},{9,13},{10,... | collective-permute-start | bytes 196616 | tf_op jit(solution)/shard_map/ppermute | solution.py:351
  8.6 14.4 %collective-permute-start.4 = (bf16[32,1920]{1,0:T(8,128)(2,1)}, bf16[32,1920]{1,0:T(8,128)(2,1)S(1)}, u32[]{:S(2)}, u32[]{:S(2)}) collective-permute-start(bf16[32,1920]{1,0:T(8,128)(2,1)} %get-tuple-element.108), channel_id=1, source_target_pairs={{0,2},{1,3},{2,0},{3,1},{4,6},{5,7},{6,4},{7,5},{8,10},{9,11},{10,... | collective-permute-start | bytes 368648 | tf_op jit(solution)/shard_map/ppermute | solution.py:351
  23.7 19.6 %collective-permute-start.1 = (bf16[128,1024]{1,0:T(8,128)(2,1)S(1)}, bf16[128,1024]{1,0:T(8,128)(2,1)S(1)}, u32[]{:S(2)}, u32[]{:S(2)}) collective-permute-start(bf16[128,1024]{1,0:T(8,128)(2,1)S(1)} %get-tuple-element.276), channel_id=1, source_target_pairs={{0,4},{1,12},{2,6},{3,14},{4,0},{5,8},{6,2},{7,10},{8,5},{9,13},{1... | collective-permute-start | bytes 786440 | tf_op jit(solution)/shard_map/ppermute | solution.py:359
  28.0 20.3 %collective-permute-start.10 = (bf16[2,2,32,896]{3,2,1,0:T(8,128)(2,1)S(1)}, bf16[2,2,32,896]{3,2,1,0:T(8,128)(2,1)S(1)}, u32[]{:S(2)}, u32[]{:S(2)}) collective-permute-start(bf16[2,2,32,896]{3,2,1,0:T(8,128)(2,1)S(1)} %pad_maximum_fusion.26), channel_id=1, source_target_pairs={{0,4},{1,5},{2,6},{3,7},{4,0},{5,1},{6,2},{7,3},{8,12},{9,13},{10,... | collective-permute-start | bytes 688136 | tf_op jit(solution)/shard_map/ppermute | solution.py:351
  44.1 22.3 %collective-permute-start.2 = (bf16[256,1024]{1,0:T(8,128)(2,1)S(1)}, bf16[256,1024]{1,0:T(8,128)(2,1)S(1)}, u32[]{:S(2)}, u32[]{:S(2)}) collective-permute-start(bf16[256,1024]{1,0:T(8,128)(2,1)S(1)} %fusion.9), channel_id=1, source_target_pairs={{0,2},{1,3},{2,0},{3,1},{4,6},{5,7},{6,4},{7,5},{8,10},{9,11},{10,... | collective-permute-start | bytes 1572872 | tf_op jit(solution)/shard_map/ppermute | solution.py:351
  48.4 18.2 %collective-permute-start.17 = (bf16[128,1024]{1,0:T(8,128)(2,1)S(1)}, bf16[128,1024]{1,0:T(8,128)(2,1)S(1)}, u32[]{:S(2)}, u32[]{:S(2)}) collective-permute-start(bf16[128,1024]{1,0:T(8,128)(2,1)S(1)} %copy-done.25), channel_id=1, source_target_pairs={{0,4},{1,5},{2,6},{3,7},{4,0},{5,1},{6,2},{7,3},{8,12},{9,13},{10,... | collective-permute-start | bytes 786440 | tf_op jit(solution)/shard_map/ppermute | solution.py:351
  71.7 23.0 %collective-permute-start.22 = (bf16[256,1024]{1,0:T(8,128)(2,1)S(1)}, bf16[256,1024]{1,0:T(8,128)(2,1)}, u32[]{:S(2)}, u32[]{:S(2)}) collective-permute-start(bf16[256,1024]{1,0:T(8,128)(2,1)S(1)} %constant_dynamic-update-slice_fusion), channel_id=1, source_target_pairs={{0,2},{1,3},{2,0},{3,1},{4,6},{5,7},{6,4},{7,5},{8,10},{9,11},{10,... | collective-permute-start | bytes 1572872 | tf_op jit(solution)/shard_map/ppermute | solution.py:351
  77.7 19.8 %collective-permute-start.20 = (bf16[2,64,1024]{2,1,0:T(8,128)(2,1)}, bf16[2,64,1024]{2,1,0:T(8,128)(2,1)}, u32[]{:S(2)}, u32[]{:S(2)}) collective-permute-start(bf16[2,64,1024]{2,1,0:T(8,128)(2,1)} %get-tuple-element.268), channel_id=1, source_target_pairs={{0,16},{1,17},{2,18},{3,19},{4,20},{5,21},{6,22},{7,23},{8,24},{9,... | collective-permute-start | bytes 786440 | tf_op jit(solution)/shard_map/ppermute | solution.py:351
  78.5 19.0 %collective-permute-start.21 = (bf16[2,64,1024]{2,1,0:T(8,128)(2,1)}, bf16[2,64,1024]{2,1,0:T(8,128)(2,1)}, u32[]{:S(2)}, u32[]{:S(2)}) collective-permute-start(bf16[2,64,1024]{2,1,0:T(8,128)(2,1)} %get-tuple-element.267), channel_id=1, source_target_pairs={{0,1},{1,0},{2,3},{3,2},{4,5},{5,4},{6,7},{7,6},{8,9},{9,8},{10,11... | collective-permute-start | bytes 786440 | tf_op jit(solution)/shard_map/ppermute | solution.py:351
  80.2 17.3 %collective-permute-start.18 = (bf16[2,2,2,32,1024]{4,3,2,1,0:T(8,128)(2,1)S(1)}, bf16[2,2,2,32,1024]{4,3,2,1,0:T(8,128)(2,1)}, u32[]{:S(2)}, u32[]{:S(2)}) collective-permute-start(bf16[2,2,2,32,1024]{4,3,2,1,0:T(8,128)(2,1)S(1)} %pad_maximum_fusion.11), channel_id=1, source_target_pairs={{0,1},{1,0},{2,3},{3,2},{4,5},{5,4},{6,7},{7,6},{8,9},{9,8},{10,11... | collective-permute-start | bytes 1572872 | tf_op jit(solution)/shard_map/ppermute | solution.py:351
  80.6 17.0 %collective-permute-start.19 = (bf16[2,2,32,1024]{3,2,1,0:T(8,128)(2,1)S(1)}, bf16[2,2,32,1024]{3,2,1,0:T(8,128)(2,1)}, u32[]{:S(2)}, u32[]{:S(2)}) collective-permute-start(bf16[2,2,32,1024]{3,2,1,0:T(8,128)(2,1)S(1)} %pad_maximum_fusion.22), channel_id=1, source_target_pairs={{0,4},{1,5},{2,6},{3,7},{4,0},{5,1},{6,2},{7,3},{8,12},{9,13},{10,... | collective-permute-start | bytes 786440 | tf_op jit(solution)/shard_map/ppermute | solution.py:351
  106.9 13.9 %collective-permute-start.33 = (bf16[2,2,2,32,1024]{4,3,2,1,0:T(8,128)(2,1)S(1)}, bf16[2,2,2,32,1024]{4,3,2,1,0:T(8,128)(2,1)S(1)}, u32[]{:S(2)}, u32[]{:S(2)}) collective-permute-start(bf16[2,2,2,32,1024]{4,3,2,1,0:T(8,128)(2,1)S(1)} %pad_maximum_fusion.16), channel_id=1, source_target_pairs={{0,1},{1,0},{2,3},{3,2},{4,5},{5,4},{6,7},{7,6},{8,9},{9,8},{10,11... | collective-permute-start | bytes 1572872 | tf_op jit(solution)/shard_map/ppermute | solution.py:351
  148.2 17.8 %collective-permute-start.36 = (bf16[256,1024]{1,0:T(8,128)(2,1)S(1)}, bf16[256,1024]{1,0:T(8,128)(2,1)S(1)}, u32[]{:S(2)}, u32[]{:S(2)}) collective-permute-start(bf16[256,1024]{1,0:T(8,128)(2,1)S(1)} %add_convert_fusion.4), channel_id=1, source_target_pairs={{0,2},{1,3},{2,0},{3,1},{4,6},{5,7},{6,4},{7,5},{8,10},{9,11},{10,... | collective-permute-start | bytes 1572872 | tf_op jit(solution)/shard_map/ppermute | solution.py:351
  170.6 25.9 %collective-permute-start.40 = (bf16[2,2,2,2,32,1024]{5,4,3,2,1,0:T(8,128)(2,1)}, bf16[2,2,2,2,32,1024]{5,4,3,2,1,0:T(8,128)(2,1)}, u32[]{:S(2)}, u32[]{:S(2)}) collective-permute-start(bf16[2,2,2,2,32,1024]{5,4,3,2,1,0:T(8,128)(2,1)} %dynamic-slice_bitcast_fusion), channel_id=1, source_target_pairs={{0,1},{1,0},{2,3},{3,2},{4,5},{5,4},{6,7},{7,6},{8,9},{9,8},{10,11... | collective-permute-start | bytes 3145736 | tf_op jit(solution)/shard_map/ppermute | solution.py:351
  172.4 25.9 %collective-permute-start.39 = (bf16[2,2,128,1024]{3,2,0,1:T(8,128)(2,1)}, bf16[2,2,128,1024]{3,2,0,1:T(8,128)(2,1)}, u32[]{:S(2)}, u32[]{:S(2)}) collective-permute-start(bf16[2,2,128,1024]{3,2,0,1:T(8,128)(2,1)} %copy_bitcast_fusion), channel_id=1, source_target_pairs={{0,16},{1,17},{2,18},{3,19},{4,20},{5,21},{6,22},{7,23},{8,24},{9,... | collective-permute-start | bytes 3145736 | tf_op jit(solution)/shard_map/ppermute | solution.py:351
  179.5 15.1 %collective-permute-start.41 = (bf16[256,1024]{1,0:T(8,128)(2,1)}, bf16[256,1024]{1,0:T(8,128)(2,1)}, u32[]{:S(2)}, u32[]{:S(2)}) collective-permute-start(bf16[256,1024]{1,0:T(8,128)(2,1)} %add_convert_fusion.3), channel_id=1, source_target_pairs={{0,2},{1,3},{2,0},{3,1},{4,6},{5,7},{6,4},{7,5},{8,10},{9,11},{10,... | collective-permute-start | bytes 1572872 | tf_op jit(solution)/shard_map/ppermute | solution.py:351
  183.1 16.3 %collective-permute-start.38 = (bf16[512,256]{1,0:T(8,128)(2,1)}, bf16[512,256]{1,0:T(8,128)(2,1)}, u32[]{:S(2)}, u32[]{:S(2)}) collective-permute-start(bf16[512,256]{1,0:T(8,128)(2,1)} %get-tuple-element.255), channel_id=1, source_target_pairs={{0,2},{1,3},{2,0},{3,1},{4,6},{5,7},{6,4},{7,5},{8,10},{9,11},{10,... | collective-permute-start | bytes 786440 | tf_op jit(solution)/shard_map/ppermute | solution.py:351
  199.5 25.8 %collective-permute-start.47 = (bf16[2,2,2,32,1024]{4,3,1,0,2:T(8,128)(2,1)S(1)}, bf16[2,2,2,32,1024]{4,3,1,0,2:T(8,128)(2,1)S(1)}, u32[]{:S(2)}, u32[]{:S(2)}) collective-permute-start(bf16[2,2,2,32,1024]{4,3,1,0,2:T(8,128)(2,1)S(1)} %dynamic-slice_bitcast_fusion.1), channel_id=1, source_target_pairs={{0,16},{1,17},{2,18},{3,19},{4,20},{5,21},{6,22},{7,23},{8,24},{9,... | collective-permute-start | bytes 1572872 | tf_op jit(solution)/shard_map/ppermute | solution.py:351
  200.1 22.0 %collective-permute-start.44 = (bf16[128,1024]{1,0:T(8,128)(2,1)S(1)}, bf16[128,1024]{1,0:T(8,128)(2,1)S(1)}, u32[]{:S(2)}, u32[]{:S(2)}) collective-permute-start(bf16[128,1024]{1,0:T(8,128)(2,1)S(1)} %get-tuple-element.253), channel_id=1, source_target_pairs={{0,0},{1,8},{2,2},{3,10},{4,4},{5,12},{6,6},{7,14},{8,1},{9,9},{10... | collective-permute-start | bytes 786440 | tf_op jit(solution)/shard_map/ppermute | solution.py:359
  200.8 21.3 %collective-permute-start.45 = (bf16[128,1024]{1,0:T(8,128)(2,1)S(1)}, bf16[128,1024]{1,0:T(8,128)(2,1)S(1)}, u32[]{:S(2)}, u32[]{:S(2)}) collective-permute-start(bf16[128,1024]{1,0:T(8,128)(2,1)S(1)} %get-tuple-element.254), channel_id=1, source_target_pairs={{0,4},{1,12},{2,6},{3,14},{4,0},{5,8},{6,2},{7,10},{8,5},{9,13},{1... | collective-permute-start | bytes 786440 | tf_op jit(solution)/shard_map/ppermute | solution.py:359
  205.0 18.2 %collective-permute-start.43 = (bf16[2,128,1024]{2,1,0:T(8,128)(2,1)S(1)}, bf16[2,128,1024]{2,1,0:T(8,128)(2,1)S(1)}, u32[]{:S(2)}, u32[]{:S(2)}) collective-permute-start(bf16[2,128,1024]{2,1,0:T(8,128)(2,1)S(1)} %dynamic-slice_bitcast_fusion.2), channel_id=1, source_target_pairs={{0,1},{1,0},{2,3},{3,2},{4,5},{5,4},{6,7},{7,6},{8,9},{9,8},{10,11... | collective-permute-start | bytes 1572872 | tf_op jit(solution)/shard_map/ppermute | solution.py:351
  210.1 13.9 %collective-permute-start.42 = (bf16[2,2,2,32,1024]{4,3,2,1,0:T(8,128)(2,1)S(1)}, bf16[2,2,2,32,1024]{4,3,2,1,0:T(8,128)(2,1)S(1)}, u32[]{:S(2)}, u32[]{:S(2)}) collective-permute-start(bf16[2,2,2,32,1024]{4,3,2,1,0:T(8,128)(2,1)S(1)} %dynamic-slice_bitcast_fusion.3), channel_id=1, source_target_pairs={{0,16},{1,17},{2,18},{3,19},{4,20},{5,21},{6,22},{7,23},{8,24},{9,... | collective-permute-start | bytes 1572872 | tf_op jit(solution)/shard_map/ppermute | solution.py:351
  229.3 26.6 %collective-permute-start.54 = (bf16[2,128,1024]{2,1,0:T(8,128)(2,1)S(1)}, bf16[2,128,1024]{2,1,0:T(8,128)(2,1)S(1)}, u32[]{:S(2)}, u32[]{:S(2)}) collective-permute-start(bf16[2,128,1024]{2,1,0:T(8,128)(2,1)S(1)} %fusion.29), channel_id=1, source_target_pairs={{0,4},{1,5},{2,6},{3,7},{4,0},{5,1},{6,2},{7,3},{8,12},{9,13},{10,... | collective-permute-start | bytes 1572872 | tf_op jit(solution)/shard_map/ppermute | solution.py:351
  232.9 16.0 %collective-permute-start.49 = (bf16[2,2,2,32,768]{4,3,2,1,0:T(8,128)(2,1)S(1)}, bf16[2,2,2,32,768]{4,3,2,1,0:T(8,128)(2,1)S(1)}, u32[]{:S(2)}, u32[]{:S(2)}) collective-permute-start(bf16[2,2,2,32,768]{4,3,2,1,0:T(8,128)(2,1)S(1)} %dynamic-slice_bitcast_fusion.5), channel_id=1, source_target_pairs={{0,1},{1,0},{2,3},{3,2},{4,5},{5,4},{6,7},{7,6},{8,9},{9,8},{10,11... | collective-permute-start | bytes 1179656 | tf_op jit(solution)/shard_map/ppermute | solution.py:351
  234.3 15.5 %collective-permute-start.51 = (bf16[2,2,2,32,768]{4,3,2,1,0:T(8,128)(2,1)S(1)}, bf16[2,2,2,32,768]{4,3,2,1,0:T(8,128)(2,1)S(1)}, u32[]{:S(2)}, u32[]{:S(2)}) collective-permute-start(bf16[2,2,2,32,768]{4,3,2,1,0:T(8,128)(2,1)S(1)} %dynamic-slice_bitcast_fusion.4), channel_id=1, source_target_pairs={{0,16},{1,17},{2,18},{3,19},{4,20},{5,21},{6,22},{7,23},{8,24},{9,... | collective-permute-start | bytes 1179656 | tf_op jit(solution)/shard_map/ppermute | solution.py:351
  235.2 23.4 %collective-permute-start.48 = (bf16[256,1024]{1,0:T(8,128)(2,1)S(1)}, bf16[256,1024]{1,0:T(8,128)(2,1)S(1)}, u32[]{:S(2)}, u32[]{:S(2)}) collective-permute-start(bf16[256,1024]{1,0:T(8,128)(2,1)S(1)} %add_convert_fusion.1), channel_id=1, source_target_pairs={{0,2},{1,3},{2,0},{3,1},{4,6},{5,7},{6,4},{7,5},{8,10},{9,11},{10,... | collective-permute-start | bytes 1572872 | tf_op jit(solution)/shard_map/ppermute | solution.py:351
  260.5 21.5 %collective-permute-start.57 = (bf16[2,2,32,768]{3,2,1,0:T(8,128)(2,1)S(1)}, bf16[2,2,32,768]{3,2,1,0:T(8,128)(2,1)S(1)}, u32[]{:S(2)}, u32[]{:S(2)}) collective-permute-start(bf16[2,2,32,768]{3,2,1,0:T(8,128)(2,1)S(1)} %dynamic-slice_bitcast_fusion.11), channel_id=1, source_target_pairs={{0,4},{1,5},{2,6},{3,7},{4,0},{5,1},{6,2},{7,3},{8,12},{9,13},{10,... | collective-permute-start | bytes 589832 | tf_op jit(solution)/shard_map/ppermute | solution.py:351
  260.6 21.4 %collective-permute-start.58 = (bf16[2,32,1024]{2,1,0:T(8,128)(2,1)S(1)}, bf16[2,32,1024]{2,1,0:T(8,128)(2,1)S(1)}, u32[]{:S(2)}, u32[]{:S(2)}) collective-permute-start(bf16[2,32,1024]{2,1,0:T(8,128)(2,1)S(1)} %dynamic-slice_bitcast_fusion.14), channel_id=1, source_target_pairs={{0,4},{1,5},{2,6},{3,7},{4,0},{5,1},{6,2},{7,3},{8,12},{9,13},{10,... | collective-permute-start | bytes 393224 | tf_op jit(solution)/shard_map/ppermute | solution.py:351
  263.6 26.0 %collective-permute-start.55 = (bf16[128,1024]{1,0:T(8,128)(2,1)S(1)}, bf16[128,1024]{1,0:T(8,128)(2,1)S(1)}, u32[]{:S(2)}, u32[]{:S(2)}) collective-permute-start(bf16[128,1024]{1,0:T(8,128)(2,1)S(1)} %get-tuple-element.249), channel_id=1, source_target_pairs={{0,0},{1,8},{2,2},{3,10},{4,4},{5,12},{6,6},{7,14},{8,1},{9,9},{10... | collective-permute-start | bytes 786440 | tf_op jit(solution)/shard_map/ppermute | solution.py:359
  264.3 25.3 %collective-permute-start.56 = (bf16[128,1024]{1,0:T(8,128)(2,1)S(1)}, bf16[128,1024]{1,0:T(8,128)(2,1)S(1)}, u32[]{:S(2)}, u32[]{:S(2)}) collective-permute-start(bf16[128,1024]{1,0:T(8,128)(2,1)S(1)} %get-tuple-element.250), channel_id=1, source_target_pairs={{0,4},{1,12},{2,6},{3,14},{4,0},{5,8},{6,2},{7,10},{8,5},{9,13},{1... | collective-permute-start | bytes 786440 | tf_op jit(solution)/shard_map/ppermute | solution.py:359
  (62 other events, 661.6 us)
